TPU v7x, 32 devices: a whole 2x2x4 slice. The times are simulated.
32 devices in a mesh: groups: 2 (over y), seq: 4 (over z), head: 2 (over x), rep: 2 (over core).
Axes of the slice: x: 2, y: 2, z: 4, core: 2. Of those that a mesh axis runs over, the one named last changes fastest.
Arguments:
- query_proj: bfloat16 [2048, 4096], P(('groups', 'seq'), ('head', 'rep')), parts along dimension 0, may hold values from -6 to 6
- key_proj: bfloat16 [2048, 4096], P(('groups', 'seq'), ('head', 'rep')), parts along dimension 0, may hold values from -6 to 6
- value_proj: bfloat16 [2048, 4096], P(('groups', 'seq'), ('head', 'rep')), parts along dimension 0, may hold values from -6 to 6
- forget_logits: bfloat16 [2048, 4096], P(('groups', 'seq'), ('head', 'rep')), parts along dimension 0, may hold values from -8 to 8
- decay_rate: float32 [4096], P(('head', 'rep')), may hold values from 0.001 to 0.1
- beta_logits: bfloat16 [2048, 32], P(('groups', 'seq'), ('head', 'rep')), parts along dimension 0, may hold values from -4.5 to -0.5
- gate_logits: bfloat16 [2048, 4096], P(('groups', 'seq'), ('head', 'rep')), parts along dimension 0, may hold values from -6 to 6
- norm_gain: float32 [128], replicated, may hold values from 0.25 to 1.75
- out_weight: bfloat16 [4096, 2304], P(('head', 'rep')), may hold values from -0.125 to 0.125
- stream_starts: int32 [16], P('groups'), parts along dimension 0, may hold values from 0 to 1023, as said below
- stream_slots: int32 [16], P('groups'), parts along dimension 0, may hold values from 0 to 7, each once
Outputs:
- layer_out: bfloat16 [2048, 2304], P(('groups', 'seq'), ('head', 'rep')), parts along dimension 0
- slot_states: bfloat16 [16, 32, 128, 128], P(('groups', 'seq'), ('head', 'rep')), parts along dimension 0
There are 2 independent parts, one for each index of `groups`. A program takes and returns all parts, laid end to end along the dimension named above; an argument that names none is the same for every part. Nothing has to cross between parts.
Inputs may be any that keep to these rules, and one draw needn't show every extreme that they name: `stream_starts`: strictly increasing, the first is 0; at most 4 streams end within one index of seq's 256 tokens, and in every draw some index has exactly 4 ends. `stream_slots`: each slot once; slot s is kept by index s // 2 of seq.
All inputs are finite; a program needn't handle non-finite values.
Results may differ from a plain program's by a relative error of at most 0.014.
Values may be sent and summed in bfloat16 or wider, within the bound.
A program may use at most 64 MiB of HBM per device.

v0:
```python
import jax
import jax.numpy as jnp
from jax import lax
from jax.sharding import PartitionSpec as P

ENDS_MAX = 4


SMALLEST_STEP = lax.Precision.HIGHEST


def from_behind(block, axis, distance):
    devices = range(lax.axis_size(axis))
    route = [(i - distance, i) for i in devices if i - distance in devices]
    return lax.ppermute(block, axis, route)


def exact_matmul(left, right):
    return jnp.matmul(left, right, precision=SMALLEST_STEP)


def unit_heads(rows, head_count, row_width):
    shaped = rows.astype(jnp.float32).reshape(rows.shape[0], head_count, row_width)
    shaped = shaped * lax.rsqrt(jnp.sum(shaped * shaped, axis=-1, keepdims=True) + 1e-06)
    return shaped.transpose(1, 0, 2)


def to_blocks(tensor, blocks):
    head_count, length, row_width = tensor.shape
    return tensor.reshape(head_count, blocks, length // blocks, row_width).transpose(1, 0, 2, 3)


def run_blocks(inputs, initial):
    head_count, block_len, key_width = inputs[0].shape[1:]
    value_width = inputs[2].shape[-1]
    end_count = inputs[7].shape[1]
    identity = jnp.broadcast_to(
        jnp.eye(key_width, dtype=jnp.float32), (head_count, key_width, key_width)
    )
    row_index = jnp.arange(block_len)[:, None]
    column_index = jnp.arange(block_len)[None, :]

    def advance(carry, slices):
        current, prefix, end_states, end_maps = carry
        query_blk, key_blk, value_blk, decay_blk, beta_blk, segment_blk, first_blk, select_blk = (
            slices
        )
        cumulative = jnp.cumsum(decay_blk, axis=1)
        center = 0.5 * (cumulative[:, :1, :] + cumulative[:, -1:, :])
        rising = jnp.exp(cumulative - center)
        falling = jnp.exp(center - cumulative)
        decayed = jnp.exp(cumulative)
        key_up = key_blk * rising
        key_down = key_blk * falling
        query_up = query_blk * rising
        same_stream = segment_blk[:, None] == segment_blk[None, :]
        strict = (same_stream & (row_index > column_index)).astype(jnp.float32)
        up_to_self = (same_stream & (row_index >= column_index)).astype(jnp.float32)
        coupling = jnp.einsum("htd,hsd->hts", key_up, key_down, precision=SMALLEST_STEP) * (
            beta_blk[:, :, None] * strict
        )
        reading = (
            jnp.einsum("htd,hsd->hts", query_up, key_down, precision=SMALLEST_STEP) * up_to_self
        )
        start_mask = first_blk[None, :, None]
        right_side = jnp.concatenate(
            [
                value_blk * beta_blk[:, :, None],
                key_blk * decayed * (beta_blk[:, :, None] * start_mask),
            ],
            axis=-1,
        )
        solved = lax.linalg.triangular_solve(
            coupling, right_side, left_side=True, lower=True, unit_diagonal=True
        )
        value_part = solved[..., :value_width]
        key_part = solved[..., value_width:]
        state_updates = value_part - exact_matmul(key_part, current)
        last_same = (segment_blk == segment_blk[-1]).astype(jnp.float32)
        tail_decay = jnp.exp(cumulative[:, -1:, :] - cumulative)
        key_remainder = key_blk * tail_decay * last_same[None, :, None]
        keep_first = first_blk[-1]
        decay_end = decayed[:, -1, :]
        next_state = keep_first * decay_end[:, :, None] * current + jnp.einsum(
            "pmu,pmo->puo", key_remainder, state_updates, precision=SMALLEST_STEP
        )
        transfer = keep_first * (decay_end[:, :, None] * identity) - jnp.einsum(
            "hsk,hsj->hkj", key_remainder, key_part, precision=SMALLEST_STEP
        )
        new_prefix = exact_matmul(transfer, prefix)
        emitted = ()
        query_start = query_blk * decayed * start_mask
        outputs = exact_matmul(query_start, current) + exact_matmul(reading, state_updates)
        end_reach = jnp.dot(select_blk, up_to_self, precision=SMALLEST_STEP)
        end_up = jnp.einsum("et,htd->ehd", select_blk, rising, precision=SMALLEST_STEP)
        end_true = jnp.einsum("et,htd->ehd", select_blk, decayed, precision=SMALLEST_STEP)
        end_first = jnp.dot(select_blk, first_blk, precision=SMALLEST_STEP)
        key_end = end_reach[:, None, :, None] * end_up[:, :, None, :] * key_down[None]
        end_states = (
            end_states
            + end_first[:, None, None, None] * end_true[..., None] * current[None]
            + jnp.einsum("ehsk,hsv->ehkv", key_end, state_updates, precision=SMALLEST_STEP)
        )
        corrections = exact_matmul(query_start - exact_matmul(reading, key_part), prefix)
        end_map_blk = end_first[:, None, None, None] * (
            end_true[..., None] * identity[None]
        ) - jnp.einsum("ehsk,hsj->ehkj", key_end, key_part, precision=SMALLEST_STEP)
        end_maps = end_maps + jnp.einsum(
            "ehkj,hjm->ehkm", end_map_blk, prefix, precision=SMALLEST_STEP
        )
        emitted = (outputs, corrections)
        return ((next_state, new_prefix, end_states, end_maps), emitted)

    starting = (
        initial,
        identity,
        jnp.zeros((end_count, head_count, key_width, value_width), jnp.float32),
        jnp.zeros((end_count, head_count, key_width, key_width), jnp.float32),
    )
    return lax.scan(advance, starting, inputs)


def per_device(
    query_proj,
    key_proj,
    value_proj,
    forget_logits,
    decay_rate,
    beta_logits,
    gate_logits,
    norm_gain,
    out_weight,
    stream_starts,
    stream_slots,
):
    length = query_proj.shape[0]
    head_count = beta_logits.shape[1]
    key_width = decay_rate.shape[0] // head_count
    value_width = value_proj.shape[1] // head_count
    devices = lax.axis_size("seq")
    seq_place = lax.axis_index("seq")
    anchor = seq_place * length
    pack_len = length * devices
    block_len = min(128, length)
    blocks = length // block_len
    queries = unit_heads(query_proj, head_count, key_width)
    keys_unit = unit_heads(key_proj, head_count, key_width)
    values_all = (
        value_proj.astype(jnp.float32).reshape(length, head_count, value_width).transpose(1, 0, 2)
    )
    softened = jax.nn.softplus(
        forget_logits.astype(jnp.float32).reshape(length, head_count, key_width).transpose(1, 0, 2)
    )
    log_decay = -(decay_rate.reshape(head_count, 1, key_width) * softened)
    betas = jax.nn.sigmoid(beta_logits.astype(jnp.float32)).T
    token_positions = anchor + jnp.arange(length, dtype=jnp.int32)
    segments = jnp.sum(
        (stream_starts[None, :] <= token_positions[:, None]).astype(jnp.int32), axis=1
    )
    block_begin = anchor + block_len * jnp.arange(blocks, dtype=jnp.int32)
    before_blocks = jnp.sum(
        (stream_starts[None, :] <= block_begin[:, None] - 1).astype(jnp.int32), axis=1
    )
    firsts = (segments.reshape(blocks, block_len) == before_blocks[:, None]).astype(jnp.float32)
    stream_ends = jnp.concatenate([stream_starts[1:] - 1, jnp.full((1,), pack_len - 1, jnp.int32)])
    local_ends = stream_ends - anchor
    within_flags = (local_ends >= 0) & (local_ends < length)
    earlier = jnp.sum((stream_ends < anchor).astype(jnp.int32))
    stream_rank = jnp.arange(stream_starts.shape[0], dtype=jnp.int32) - earlier
    matches = within_flags[None, :] & (
        stream_rank[None, :] == jnp.arange(ENDS_MAX, dtype=jnp.int32)[:, None]
    )
    end_places = jnp.sum(jnp.where(matches, local_ends[None, :], 0), axis=1)
    end_valid = jnp.any(matches, axis=1)
    end_slots = jnp.where(
        end_valid, jnp.sum(jnp.where(matches, stream_slots[None, :], 0), axis=1), -1
    )
    selects = (
        (end_places[:, None] == jnp.arange(length, dtype=jnp.int32)[None, :]) & end_valid[:, None]
    ).astype(jnp.float32)
    inputs = (
        to_blocks(queries, blocks),
        to_blocks(keys_unit, blocks),
        to_blocks(values_all, blocks),
        to_blocks(log_decay, blocks),
        betas.reshape(head_count, blocks, block_len).transpose(1, 0, 2),
        segments.reshape(blocks, block_len),
        firsts,
        selects.reshape(ENDS_MAX, blocks, block_len).transpose(1, 0, 2),
    )
    zero_state = jnp.zeros((head_count, key_width, value_width), jnp.float32)
    carried, emitted = run_blocks(inputs, zero_state)
    transfer = carried[1]
    summary = carried[0]

    def relay(turn_index, arriving_state):
        return from_behind(
            (exact_matmul(transfer, arriving_state) + summary).astype(jnp.bfloat16), "seq", 1
        ).astype(jnp.float32)

    arriving = lax.fori_loop(0, devices - 1, relay, jnp.zeros_like(summary))
    outputs = emitted[0] + exact_matmul(emitted[1], arriving[None])
    end_states = carried[2] + jnp.einsum(
        "ehkj,hjv->ehkv", carried[3], arriving, precision=SMALLEST_STEP
    )
    outputs = outputs.transpose(0, 2, 1, 3).reshape(length, head_count, value_width)
    inverse_rms = lax.rsqrt(jnp.mean(outputs * outputs, axis=-1, keepdims=True) + 1e-05)
    gates = jax.nn.sigmoid(gate_logits.astype(jnp.float32).reshape(length, head_count, value_width))
    hidden = (
        (outputs * inverse_rms * norm_gain * gates)
        .reshape(length, head_count * value_width)
        .astype(jnp.bfloat16)
    )
    partial_value = jnp.dot(hidden, out_weight, preferred_element_type=jnp.float32)
    layer_out = lax.psum_scatter(
        partial_value.astype(jnp.bfloat16), ("head", "rep"), scatter_dimension=1, tiled=True
    )
    packed = end_states.astype(jnp.bfloat16)
    owned_slots = stream_slots.shape[0] // devices
    slot_base = seq_place * owned_slots
    states_piece = lax.all_gather(packed, "seq", axis=0, tiled=True)
    slots_piece = lax.all_gather(end_slots, "seq", axis=0, tiled=True)
    chosen = (
        slots_piece[None, :] == slot_base + jnp.arange(owned_slots, dtype=jnp.int32)[:, None]
    ).astype(jnp.bfloat16)
    flattened = states_piece.reshape(states_piece.shape[0], -1)
    collected = jnp.dot(chosen, flattened, preferred_element_type=jnp.float32).reshape(
        jnp.zeros((owned_slots, head_count, key_width, value_width), jnp.float32).shape
    )
    slot_states = collected.astype(jnp.bfloat16)
    return (layer_out, slot_states)


def solution(mesh):
    in_specs = (
        P(("groups", "seq"), ("head", "rep")),
        P(("groups", "seq"), ("head", "rep")),
        P(("groups", "seq"), ("head", "rep")),
        P(("groups", "seq"), ("head", "rep")),
        P(("head", "rep")),
        P(("groups", "seq"), ("head", "rep")),
        P(("groups", "seq"), ("head", "rep")),
        P(),
        P(("head", "rep"), None),
        P("groups"),
        P("groups"),
    )
    out_specs = (
        P(("groups", "seq"), ("head", "rep")),
        P(("groups", "seq"), ("head", "rep"), None, None),
    )
    return jax.shard_map(
        per_device, mesh=mesh, in_specs=in_specs, out_specs=out_specs, check_vma=False
    )
```

profile of v0, /device:TPU:0, one launch (start us, length us, event | category | flops | bytes accessed | tf_op | source)
XLA Modules:
  0.0 429.4 jit_solution(6693638468967164350)
XLA Ops:
  12.6 1.3 copy.186
  15.2 1.3 copy.185
  16.5 1.1 convert_bitcast_fusion.2
  18.5 1.3 broadcast_multiply_fusion.3
  19.8 1.2 convert_bitcast_fusion.1
  22.2 258.6 %while.34 = (s32[]{:T(128)}, f32[8,128,128]{2,1,0:T(8,128)}, f32[8,128,128]{2,1,0:T(8,128)S(1)}, f32[4,8,128,128]{2,3,0,1:T(8,128)}, f32[4,8,128,128]{3,2,0,1:T(...) while((s32[]{:T(128)}, f32[8,128,128]{2,1,0:T(8,128)}, ...), condition=%wide.region_9.10_spmd.clone.clone, body=%wide.region_7.9_spmd.clone.clone.sunk | while | flops 4874140160 | bytes 133568368 | solution.py:120
  42.5 0.9 copy.325
  43.4 1.5 fusion.211
  44.9 79.2 %custom-call.12 = f32[8,1,128,128]{2,3,1,0:T(8,128)} custom-call(f32[8,1,128,128]{3,2,1,0:T(8,128)S(1)} %fusion.211), custom_call_target="InvertDiagBlocksLowerTriangular" | custom-call | tf_op jit(solution)/shard_map/while/body/eval_jaxpr/triangular_solve | solution.py:73
  124.1 2.2 convolution_multiply_fusion.3
  126.4 1.0 bitcast_multiply_fusion.21
  127.4 1.6 fusion.217
  129.0 1.0 copy.326
  131.2 1.1 fusion.212
  132.9 2.7 convolution_subtract_fusion.7
  135.6 2.6 convolution_subtract_fusion.8
  138.9 2.0 convolution_add_fusion.4
  140.9 1.5 fusion.218
  142.4 2.1 copy.328
  144.5 2.1 constant_dynamic-update-slice_fusion.2
  146.6 1.5 fusion.219
  148.1 3.0 bitcast_add_fusion.5
  151.1 2.1 fusion.216
  153.4 4.4 %bitcast_add_fusion.6 = f32[4,8,128,128]{3,2,0,1:T(8,128)S(1)} fusion(f32[4,8,128,128]{3,2,0,1:T(8,128)S(1)} %copy-done.7, f32[8,128,4,128]{3,1,2,0:T(8,128)S(1)} %fusion.216, f32[128,128]{0,1:T(8,128)S(1)} %copy.327, f32[4,8,128]{2,0,1:T(4,128)S(1)} %get-tuple-element.580, f32[4]{0:T(128)S(1)} %convolution_bitcast_fusion.4, pred[]{:T(512)S(6)} %compare.11, ...), kind=kOutput, calls=%fused_computation.9.clone.1 | convolution fusion | flops 807927808 | bytes 6897681 | tf_op jit(solution)/shard_map/while/body/eval_jaxpr/ehkj,hjm->ehkm/dot_general | solution.py:108
  163.2 0.9 copy.325
  164.1 1.5 fusion.211
  165.6 79.2 %custom-call.12 = f32[8,1,128,128]{2,3,1,0:T(8,128)} custom-call(f32[8,1,128,128]{3,2,1,0:T(8,128)S(1)} %fusion.211), custom_call_target="InvertDiagBlocksLowerTriangular" | custom-call | tf_op jit(solution)/shard_map/while/body/eval_jaxpr/triangular_solve | solution.py:73
  244.8 2.2 convolution_multiply_fusion.3
  247.0 2.0 bitcast_multiply_fusion.21
  249.1 1.6 fusion.217
  250.7 1.0 copy.326
  252.9 1.1 fusion.212
  254.6 2.7 convolution_subtract_fusion.7
  257.3 2.6 convolution_subtract_fusion.8
  260.6 2.0 convolution_add_fusion.4
  262.6 1.5 fusion.218
  264.1 2.1 copy.328
  266.2 2.1 constant_dynamic-update-slice_fusion.2
  268.3 1.5 fusion.219
  269.7 3.0 bitcast_add_fusion.5
  272.8 2.1 fusion.216
  275.1 4.4 %bitcast_add_fusion.6 = f32[4,8,128,128]{3,2,0,1:T(8,128)S(1)} fusion(f32[4,8,128,128]{3,2,0,1:T(8,128)S(1)} %copy-done.7, f32[8,128,4,128]{3,1,2,0:T(8,128)S(1)} %fusion.216, f32[128,128]{0,1:T(8,128)S(1)} %copy.327, f32[4,8,128]{2,0,1:T(4,128)S(1)} %get-tuple-element.580, f32[4]{0:T(128)S(1)} %convolution_bitcast_fusion.4, pred[]{:T(512)S(6)} %compare.11, ...), kind=kOutput, calls=%fused_computation.9.clone.1 | convolution fusion | flops 807927808 | bytes 6897681 | tf_op jit(solution)/shard_map/while/body/eval_jaxpr/ehkj,hjm->ehkm/dot_general | solution.py:108
  281.6 36.4 %while.33 = (s32[]{:T(128)}, f32[8,128,128]{2,1,0:T(8,128)}, f32[8,128,128]{2,1,0:T(8,128)}, f32[8,128,128]{2,1,0:T(8,128)}, s32[]{:T(128)}, /*index=5*/s32[]{:T(128)}) while((s32[]{:T(128)}, f32[8,128,128]{2,1,0:T(8,128)}, f32[8,128,128]{2,1,0:T(8,128)}, f32[8,128,128]{2,1,0:T(8,128)}, s32[]{:T(128)}, ...), condition=%wide.region_11.12_spmd.clone, body=%wide.region_10.11_spmd.clone.sunk | while | flops 201850880 | bytes 3670135 | solution.py:201
  281.6 2.0 fusion.179
  283.6 5.0 %collective-permute-start = (bf16[8,128,128]{2,1,0:T(8,128)(2,1)S(1)}, bf16[8,128,128]{2,1,0:T(8,128)(2,1)S(1)}, u32[]{:S(2)}, u32[]{:S(2)}) collective-permute-start(bf16[8,128,128]{2,1,0:T(8,128)(2,1)S(1)} %fusion.179), channel_id=1, source_target_pairs={{0,4},{4,8},{8,12},{1,5},{5,9},{9,13},{2,6},{6,10},{10,14},{3,7},{... | collective-permute-start | bytes 786440 | tf_op jit(solution)/shard_map/while/body/eval_jaxpr/ppermute | solution.py:15
  288.6 5.5 %collective-permute-done = bf16[8,128,128]{2,1,0:T(8,128)(2,1)S(1)} collective-permute-done((bf16[8,128,128]{2,1,0:T(8,128)(2,1)S(1)}, bf16[8,128,128]{2,1,0:T(8,128)(2,1)S(1)}, u32[]{:S(2)}, u32[]{:S(2)}) %collective-permute-start) | collective-permute-done | bytes 262176 | tf_op jit(solution)/shard_map/while/body/eval_jaxpr/ppermute | solution.py:15
  294.1 0.8 convert_element_type.121
  295.0 2.0 fusion.179
  297.0 4.4 %collective-permute-start = (bf16[8,128,128]{2,1,0:T(8,128)(2,1)S(1)}, bf16[8,128,128]{2,1,0:T(8,128)(2,1)S(1)}, u32[]{:S(2)}, u32[]{:S(2)}) collective-permute-start(bf16[8,128,128]{2,1,0:T(8,128)(2,1)S(1)} %fusion.179), channel_id=1, source_target_pairs={{0,4},{4,8},{8,12},{1,5},{5,9},{9,13},{2,6},{6,10},{10,14},{3,7},{... | collective-permute-start | bytes 786440 | tf_op jit(solution)/shard_map/while/body/eval_jaxpr/ppermute | solution.py:15
  301.4 4.7 %collective-permute-done = bf16[8,128,128]{2,1,0:T(8,128)(2,1)S(1)} collective-permute-done((bf16[8,128,128]{2,1,0:T(8,128)(2,1)S(1)}, bf16[8,128,128]{2,1,0:T(8,128)(2,1)S(1)}, u32[]{:S(2)}, u32[]{:S(2)}) %collective-permute-start) | collective-permute-done | bytes 262176 | tf_op jit(solution)/shard_map/while/body/eval_jaxpr/ppermute | solution.py:15
  306.0 0.8 convert_element_type.121
  306.9 2.0 fusion.179
  308.9 4.4 %collective-permute-start = (bf16[8,128,128]{2,1,0:T(8,128)(2,1)S(1)}, bf16[8,128,128]{2,1,0:T(8,128)(2,1)S(1)}, u32[]{:S(2)}, u32[]{:S(2)}) collective-permute-start(bf16[8,128,128]{2,1,0:T(8,128)(2,1)S(1)} %fusion.179), channel_id=1, source_target_pairs={{0,4},{4,8},{8,12},{1,5},{5,9},{9,13},{2,6},{6,10},{10,14},{3,7},{... | collective-permute-start | bytes 786440 | tf_op jit(solution)/shard_map/while/body/eval_jaxpr/ppermute | solution.py:15
  313.3 3.9 collective-permute-done
  317.2 0.8 convert_element_type.121
  318.0 4.8 %fusion.85 = bf16[4,8,128,128]{2,3,0,1:T(8,128)(2,1)} fusion(f32[4,8,128,128]{2,3,0,1:T(8,128)} %get-tuple-element.135, f32[4,8,128,128]{3,2,0,1:T(8,128)S(1)} %copy-done.9, f32[8,128,128]{2,1,0:T(8,128)} %get-tuple-element.134), kind=kOutput, calls=%fused_computation.128 | convolution fusion | flops 806354944 | bytes 5767168 | tf_op jit(solution)/shard_map/ehkj,hjv->ehkv/dot_general | solution.py:203
  322.9 2.7 multiply_reduce_fusion
  326.6 5.6 %convolution_convert_fusion = bf16[256,2304]{0,1:T(8,128)(2,1)} fusion(bf16[1024,2304]{1,0:T(8,128)(2,1)} %param.23, f32[32,8,8,128]{3,2,1,0:T(8,128)S(1)} %bitcast.341, f32[32,8,8,128]{3,2,1,0:T(8,128)S(1)} %bitcast.342, bf16[256,1024]{1,0:T(8,128)(2,1)S(1)} %copy-done.27, f32[1024]{0:T(1024)S(1)} %broadcast_bitcast_fusion), kind=kOutput, calls=%fused_computation.125 | convolution fusion | flops 1210646528 | bytes 8523776 | tf_op jit(solution)/shard_map/dot_general | solution.py:214
  333.6 9.9 %all-reduce = s32[16]{0:T(128)S(1)} all-reduce(s32[16]{0:T(128)S(1)} %select_dynamic-update-slice_fusion), channel_id=1, replica_groups=mesh['groups'=2,'seq'=4,'head'=2,'rep'=2] {'seq'}, use_global_device_ids=true, to_apply=%add | all-reduce | flops 16 | bytes 128
  343.5 62.5 %all-gather.2.cloned.1.call-done = bf16[16,8,128,128]{2,3,0,1:T(8,128)(2,1)} async-done(((bf16[4,8,128,128]{2,3,0,1:T(8,128)(2,1)}), bf16[16,8,128,128]{2,3,0,1:T(8,128)(2,1)}) %all-gather.2.cloned.1.call-update) | async-done | bytes 4194320 | tf_op jit(solution)/shard_map/all_gather | solution.py:221
  406.0 6.6 %copy.196 = bf16[16,8,128,128]{3,2,1,0:T(8,128)(2,1)} copy(bf16[16,8,128,128]{2,3,0,1:T(8,128)(2,1)} %all-gather.2.cloned.1.call-done) | data formatting | bytes 8388608 | tf_op jit(solution)/shard_map/all_gather | solution.py:221
  412.6 4.9 %copy.288 = bf16[2,8,1024,128]{3,1,2,0:T(8,128)(2,1)S(1)} copy(bf16[2,8,1024,128]{3,2,1,0:T(8,128)(2,1)} %bitcast.335) | data formatting | bytes 8388608
  418.2 2.6 fusion.88
  420.8 0.9 copy.198
  (198 shorter events, 27.1 us)
Async XLA Ops:
  8.0 318.2 %copy-start = (f32[128]{0:T(128)S(1)}, f32[128]{0:T(128)}, u32[]{:S(2)}) copy-start(f32[128]{0:T(128)} %param.22) | copy-start | bytes 1540
  8.0 398.0 %all-gather.2.cloned.1.call-start = ((), (), s32[]{:S(2)}) async-start(), calls=%async_computation.2 | async-start | bytes 5242880 | tf_op jit(solution)/shard_map/all_gather | solution.py:221
  13.8 1.0 copy-start.24
  19.8 1.5 copy-start.26
  19.8 1.7 copy-start.25
  38.4 4.0 copy-start.21
  38.5 88.9 %copy-start.5 = (f32[2,8,128,128]{3,2,0,1:T(8,128)}, f32[2,8,128,128]{3,2,0,1:T(8,128)S(1)}, u32[]{:S(2)}) copy-start(f32[2,8,128,128]{3,2,0,1:T(8,128)S(1)} %get-tuple-element.632) | copy-start | bytes 3145732 | tf_op jit(solution)/shard_map/while
  41.2 1.2 copy-start.20
  124.1 2.2 copy-start.23
  130.0 1.0 copy-start.15
  130.0 1.2 copy-start.19
  131.2 4.4 %copy-start.3 = (f32[8,128,128]{2,1,0:T(8,128)S(1)}, f32[8,128,128]{2,1,0:T(8,128)}, u32[]{:S(2)}) copy-start(f32[8,128,128]{2,1,0:T(8,128)} %convolution_multiply_fusion.3) | copy-start | bytes 1572868 | tf_op jit(solution)/shard_map/while
  138.2 2.7 copy-start.16
  138.9 2.0 copy-start.1
  140.9 5.7 %copy-start.13 = (f32[8,128,128]{2,1,0:T(8,128)S(1)}, f32[8,128,128]{2,1,0:T(8,128)}, u32[]{:S(2)}) copy-start(f32[8,128,128]{2,1,0:T(8,128)} %convolution_subtract_fusion.8) | copy-start | bytes 1572868 | tf_op jit(solution)/shard_map/while
  142.4 5.7 %copy-start.2 = (f32[8,128,128]{2,1,0:T(8,128)S(1)}, f32[8,128,128]{2,1,0:T(8,128)}, u32[]{:S(2)}) copy-start(f32[8,128,128]{2,1,0:T(8,128)} %copy-done.1) | copy-start | bytes 1572868 | tf_op jit(solution)/shard_map/while
  142.4 5.7 %copy-start.4 = (f32[8,128,128]{2,1,0:T(8,128)S(1)}, f32[8,128,128]{2,1,0:T(8,128)}, u32[]{:S(2)}) copy-start(f32[8,128,128]{2,1,0:T(8,128)} %copy.325) | copy-start | bytes 1572868 | tf_op jit(solution)/shard_map/while
  144.5 3.5 copy-start.10
  144.5 3.6 copy-start.17
  151.1 6.7 %copy-start.11 = (f32[4,8,128,128]{2,3,0,1:T(8,128)}, f32[4,8,128,128]{2,3,0,1:T(8,128)S(1)}, u32[]{:S(2)}) copy-start(f32[4,8,128,128]{2,3,0,1:T(8,128)S(1)} %bitcast_add_fusion.5) | copy-start | bytes 6291460 | tf_op jit(solution)/shard_map/while
  151.1 2.3 copy-start.7
  153.4 4.4 %copy-start.14 = (f32[8,128,128]{2,1,0:T(8,128)S(1)}, f32[8,128,128]{2,1,0:T(8,128)}, u32[]{:S(2)}) copy-start(f32[8,128,128]{2,1,0:T(8,128)} %convolution_subtract_fusion.7) | copy-start | bytes 1572868 | tf_op jit(solution)/shard_map/while
  153.4 5.7 %copy-start.6 = (f32[2,8,128,128]{3,2,0,1:T(8,128)S(1)}, f32[2,8,128,128]{3,2,0,1:T(8,128)}, u32[]{:S(2)}) copy-start(f32[2,8,128,128]{3,2,0,1:T(8,128)} %copy-done.5) | copy-start | bytes 3145732 | tf_op jit(solution)/shard_map/while
  153.4 5.7 %copy-start.22 = (f32[2,8,128,128]{3,1,2,0:T(8,128)S(1)}, f32[2,8,128,128]{3,1,2,0:T(8,128)}, u32[]{:S(2)}) copy-start(f32[2,8,128,128]{3,1,2,0:T(8,128)} %copy-done.21) | copy-start | bytes 3145732 | tf_op jit(solution)/shard_map/while
  157.8 1.3 copy-start.8
  159.1 4.0 copy-start.21
  159.1 90.0 %copy-start.5 = (f32[2,8,128,128]{3,2,0,1:T(8,128)}, f32[2,8,128,128]{3,2,0,1:T(8,128)S(1)}, u32[]{:S(2)}) copy-start(f32[2,8,128,128]{3,2,0,1:T(8,128)S(1)} %get-tuple-element.632) | copy-start | bytes 3145732 | tf_op jit(solution)/shard_map/while
  161.9 1.2 copy-start.20
  244.8 2.2 copy-start.23
  251.7 1.0 copy-start.15
  251.7 1.2 copy-start.19
  252.9 4.4 %copy-start.3 = (f32[8,128,128]{2,1,0:T(8,128)S(1)}, f32[8,128,128]{2,1,0:T(8,128)}, u32[]{:S(2)}) copy-start(f32[8,128,128]{2,1,0:T(8,128)} %convolution_multiply_fusion.3) | copy-start | bytes 1572868 | tf_op jit(solution)/shard_map/while
  259.9 2.7 copy-start.16
  260.6 2.0 copy-start.1
  262.6 5.7 %copy-start.13 = (f32[8,128,128]{2,1,0:T(8,128)S(1)}, f32[8,128,128]{2,1,0:T(8,128)}, u32[]{:S(2)}) copy-start(f32[8,128,128]{2,1,0:T(8,128)} %convolution_subtract_fusion.8) | copy-start | bytes 1572868 | tf_op jit(solution)/shard_map/while
  264.1 5.7 %copy-start.2 = (f32[8,128,128]{2,1,0:T(8,128)S(1)}, f32[8,128,128]{2,1,0:T(8,128)}, u32[]{:S(2)}) copy-start(f32[8,128,128]{2,1,0:T(8,128)} %copy-done.1) | copy-start | bytes 1572868 | tf_op jit(solution)/shard_map/while
  264.1 5.7 %copy-start.4 = (f32[8,128,128]{2,1,0:T(8,128)S(1)}, f32[8,128,128]{2,1,0:T(8,128)}, u32[]{:S(2)}) copy-start(f32[8,128,128]{2,1,0:T(8,128)} %copy.325) | copy-start | bytes 1572868 | tf_op jit(solution)/shard_map/while
  266.2 3.5 copy-start.10
  266.2 3.5 copy-start.17
  272.7 6.7 %copy-start.11 = (f32[4,8,128,128]{2,3,0,1:T(8,128)}, f32[4,8,128,128]{2,3,0,1:T(8,128)S(1)}, u32[]{:S(2)}) copy-start(f32[4,8,128,128]{2,3,0,1:T(8,128)S(1)} %bitcast_add_fusion.5) | copy-start | bytes 6291460 | tf_op jit(solution)/shard_map/while
  272.8 2.3 copy-start.7
  275.1 4.4 %copy-start.14 = (f32[8,128,128]{2,1,0:T(8,128)S(1)}, f32[8,128,128]{2,1,0:T(8,128)}, u32[]{:S(2)}) copy-start(f32[8,128,128]{2,1,0:T(8,128)} %convolution_subtract_fusion.7) | copy-start | bytes 1572868 | tf_op jit(solution)/shard_map/while
  275.1 5.7 %copy-start.6 = (f32[2,8,128,128]{3,2,0,1:T(8,128)S(1)}, f32[2,8,128,128]{3,2,0,1:T(8,128)}, u32[]{:S(2)}) copy-start(f32[2,8,128,128]{3,2,0,1:T(8,128)} %copy-done.5) | copy-start | bytes 3145732 | tf_op jit(solution)/shard_map/while
  275.1 5.7 %copy-start.22 = (f32[2,8,128,128]{3,1,2,0:T(8,128)S(1)}, f32[2,8,128,128]{3,1,2,0:T(8,128)}, u32[]{:S(2)}) copy-start(f32[2,8,128,128]{3,1,2,0:T(8,128)} %copy-done.21) | copy-start | bytes 3145732 | tf_op jit(solution)/shard_map/while
  279.5 1.3 copy-start.8
  280.8 0.8 copy-start.12
  281.6 36.4 %copy-start.9 = (f32[4,8,128,128]{3,2,0,1:T(8,128)S(1)}, f32[4,8,128,128]{3,2,0,1:T(8,128)}, u32[]{:S(2)}) copy-start(f32[4,8,128,128]{3,2,0,1:T(8,128)} %get-tuple-element.136) | copy-start | bytes 6291460
  283.6 10.5 %collective-permute-start = (bf16[8,128,128]{2,1,0:T(8,128)(2,1)S(1)}, bf16[8,128,128]{2,1,0:T(8,128)(2,1)S(1)}, u32[]{:S(2)}, u32[]{:S(2)}) collective-permute-start(bf16[8,128,128]{2,1,0:T(8,128)(2,1)S(1)} %fusion.179), channel_id=1, source_target_pairs={{0,4},{4,8},{8,12},{1,5},{5,9},{9,13},{2,6},{6,10},{10,14},{3,7},{... | collective-permute-start | bytes 786440 | tf_op jit(solution)/shard_map/while/body/eval_jaxpr/ppermute | solution.py:15
  297.0 9.1 %collective-permute-start = (bf16[8,128,128]{2,1,0:T(8,128)(2,1)S(1)}, bf16[8,128,128]{2,1,0:T(8,128)(2,1)S(1)}, u32[]{:S(2)}, u32[]{:S(2)}) collective-permute-start(bf16[8,128,128]{2,1,0:T(8,128)(2,1)S(1)} %fusion.179), channel_id=1, source_target_pairs={{0,4},{4,8},{8,12},{1,5},{5,9},{9,13},{2,6},{6,10},{10,14},{3,7},{... | collective-permute-start | bytes 786440 | tf_op jit(solution)/shard_map/while/body/eval_jaxpr/ppermute | solution.py:15
  308.9 8.3 %collective-permute-start = (bf16[8,128,128]{2,1,0:T(8,128)(2,1)S(1)}, bf16[8,128,128]{2,1,0:T(8,128)(2,1)S(1)}, u32[]{:S(2)}, u32[]{:S(2)}) collective-permute-start(bf16[8,128,128]{2,1,0:T(8,128)(2,1)S(1)} %fusion.179), channel_id=1, source_target_pairs={{0,4},{4,8},{8,12},{1,5},{5,9},{9,13},{2,6},{6,10},{10,14},{3,7},{... | collective-permute-start | bytes 786440 | tf_op jit(solution)/shard_map/while/body/eval_jaxpr/ppermute | solution.py:15
  318.0 4.8 %copy-start.18 = (f32[8,128,128]{2,1,0:T(8,128)S(1)}, f32[8,128,128]{2,1,0:T(8,128)}, u32[]{:S(2)}) copy-start(f32[8,128,128]{2,1,0:T(8,128)} %get-tuple-element.134) | copy-start | bytes 1572868
  322.8 98.9 %reduce-scatter.2.cloned.1.call-start = ((), (), s32[]{:S(2)}) async-start(), calls=%async_computation.1 | async-start | bytes 1474560 | tf_op jit(solution)/shard_map/reduce_scatter | solution.py:215
  325.6 1.0 copy-start.27
  326.6 5.6 %copy-start.28 = (u32[32]{0:T(128)S(1)}, u32[32]{0:T(128)}, u32[]{:S(2)}) copy-start(u32[32]{0:T(128)} %constant.85) | copy-start | bytes 388
Sparse Core Ops, SparseCore 0:
  322.9 83.0 all-gather.1
Sparse Core Ops, SparseCore 1:
  332.3 27.7 reduce-scatter.1
where the time goes:
time: 426 us; the launch traced here: 429 us
  other arithmetic  178 us (42%)
  matrix products  78.9 us (19%)
  waiting for transfers between devices  76.5 us (18%)
  local copies, waits for them, and re-layouts  39 us (9%)
  loops' own time  16.8 us (4%)
  between operations  16.7 us (4%)
  starting transfers between devices  13.9 us (3%)
  blocking collectives  9.87 us (2%)
    another operation x6, other arithmetic, advance(): lax.linalg.triangular_solve(coupling, right_side, left_side=True, lower=T...  159 us
    all_gather x1, waiting for transfers between devices, per_device(): states_piece = lax.all_gather(packed, 'seq', axis=0, tiled=True)  62.5 us
    dot_general x16, matrix products, exact_matmul(): return jnp.matmul(left, right, precision=SMALLEST_STEP)  25.6 us
    another operation x1, loops' own time, run_blocks(): return lax.scan(advance, starting, inputs)  16.7 us
    ppermute x3, waiting for transfers between devices, from_behind(): return lax.ppermute(block, axis, route)  14 us
    ppermute x3, starting transfers between devices, from_behind(): return lax.ppermute(block, axis, route)  13.8 us
    unnamed x27, local copies, waits for them, and re-layouts  10.4 us
    unnamed x1, blocking collectives  9.87 us
  transfers between devices with their start and end apart: 5, of which 4 were waited for; matrix products, arithmetic and copies ran while one was open for 6% of the time, Pallas kernels for 0%

commit v1 on v0

v1 whole, which is shorter than its diff:
```python
import functools
import jax
import jax.numpy as jnp
from jax import lax
from jax.experimental import pallas as pl
from jax.experimental.pallas import tpu as pltpu
from jax.sharding import PartitionSpec as P

ENDS_MAX = 4
STEP_HEADS = 2
BASE = 16
F32 = jnp.float32
BF16 = jnp.bfloat16
NN = (((1,), (0,)), ((), ()))
NT = (((1,), (1,)), ((), ()))


def halves(x):
    high = x.astype(BF16)
    return high, (x - high.astype(F32)).astype(BF16)


def mm1(a, b, dims=NN):
    return lax.dot_general(a.astype(BF16), b.astype(BF16), dims, preferred_element_type=F32)


def mm3(a, b, dims=NN):
    ah, al = halves(a)
    bh, bl = halves(b)
    dot = functools.partial(lax.dot_general, dimension_numbers=dims, preferred_element_type=F32)
    return dot(ah, bh) + (dot(ah, bl) + dot(al, bh))


def unit(x):
    return x * lax.rsqrt(jnp.sum(x * x, axis=-1, keepdims=True) + 1e-06)


def block_inverses(mats):
    size = mats[0].shape[0]
    row = lax.broadcasted_iota(jnp.int32, (size, size), 0)
    col = lax.broadcasted_iota(jnp.int32, (size, size), 1)
    eye = (row == col).astype(F32)
    inside = (row // BASE) == (col // BASE)
    powers = [jnp.where(inside, m, 0.0) for m in mats]
    result = [eye - p for p in powers]
    width = 2
    while width < BASE:
        powers = [mm3(p, p) for p in powers]
        result = [r + mm3(r, p) for r, p in zip(result, powers)]
        width *= 2
    width = BASE
    while width < size:
        off = ((row // (2 * width)) == (col // (2 * width))) & ((row // width) > (col // width))
        mids = [mm3(jnp.where(off, m, 0.0), r) for m, r in zip(mats, result)]
        result = [r - mm3(r, t) for r, t in zip(result, mids)]
        width *= 2
    return result


def local_kernel(info_ref, q_ref, k_ref, v_ref, f_ref, rate_ref, beta_ref, seg_col_ref, seg_row_ref,
                 out_ref, corr_ref, map_ref, tail_ref, end0_ref, ends_ref):
    length = q_ref.shape[0]
    half = length // 2
    step = pl.program_id(0)
    width = q_ref.shape[1] // STEP_HEADS
    before = info_ref[0]
    base = info_ref[1]
    ends = info_ref[2]
    seg_col = seg_col_ref[...]
    seg_row = seg_row_ref[...]
    row = lax.broadcasted_iota(jnp.int32, (length, length), 0)
    col = lax.broadcasted_iota(jnp.int32, (length, length), 1)
    same = seg_col == seg_row
    lower = same & (row >= col)
    strict = same & (row > col)
    first = (seg_col == before).astype(F32)
    first_row = (seg_row == before).astype(F32)
    sums = jnp.concatenate([(row >= col).astype(BF16), (same & (col > row)).astype(BF16)], axis=0)
    hrow = lax.broadcasted_iota(jnp.int32, (width, width), 0)
    hcol = lax.broadcasted_iota(jnp.int32, (width, width), 1)
    eye = (hrow == hcol).astype(F32)
    beta_all = jax.nn.sigmoid(beta_ref[...].astype(F32))
    lane = lax.broadcasted_iota(jnp.int32, beta_all.shape, 1)
    any_first = jnp.max(first_row)
    select = [
        ((seg_row == base + e) & (e < ends)).astype(F32) for e in range(ENDS_MAX)
    ] + [(seg_row == base + ends).astype(F32)]
    mats = []
    kept = []
    for i in range(STEP_HEADS):
        cols = slice(i * width, (i + 1) * width)
        q = unit(q_ref[:, cols].astype(F32))
        k = unit(k_ref[:, cols].astype(F32))
        x = f_ref[:, cols].astype(F32)
        soft = jnp.maximum(x, 0.0) + jnp.log1p(jnp.exp(-jnp.abs(x)))
        decay = -(rate_ref[:, cols] * soft)
        dh, dl = halves(decay)
        both = jnp.concatenate([dh, dl], axis=1)
        summed = lax.dot_general(sums, both, NN, preferred_element_type=F32)
        summed = summed[:, :width] + summed[:, width:]
        cum = summed[:length]
        suffix = jnp.exp(summed[length:])
        decayed = jnp.exp(cum)
        beta = jnp.sum(jnp.where(lane == step * STEP_HEADS + i, beta_all, 0.0), axis=1, keepdims=True)
        mid = cum[half - 1:half]
        parts = []
        scale = []
        for b in range(2):
            piece = cum[b * half:(b + 1) * half]
            center = 0.5 * (piece[:1] + piece[-1:])
            up = jnp.exp(piece - center)
            down = jnp.exp(center - piece)
            kb = k[b * half:(b + 1) * half]
            qb = q[b * half:(b + 1) * half]
            parts.append((jnp.concatenate([kb * up, qb * up], axis=0), kb * down))
            scale.append(center)
        blocks = [mm3(parts[b][0], parts[b][1], NT) for b in range(2)]
        cross = mm3(parts[1][0] * jnp.exp(scale[1] - mid), parts[0][1] * jnp.exp(mid - scale[0]), NT)
        coupling = [
            jnp.where(strict[b * half:(b + 1) * half, b * half:(b + 1) * half], blocks[b][:half], 0.0)
            * beta[b * half:(b + 1) * half]
            for b in range(2)
        ]
        coupling_cross = jnp.where(same[half:, :half], cross[:half], 0.0) * beta[half:]
        reading0 = jnp.where(lower[:half, :half], blocks[0][half:], 0.0)
        reading1 = jnp.where(lower[half:, half:], blocks[1][half:], 0.0)
        reading_cross = jnp.where(same[half:, :half], cross[half:], 0.0)
        right = jnp.concatenate([v_ref[:, cols].astype(F32) * beta, k * decayed * (beta * first)], axis=1)
        keep_row = jnp.exp(jnp.sum(first * decay, axis=0, keepdims=True))
        mats += coupling
        kept.append((coupling_cross, reading0, reading1, reading_cross, right,
                     q * decayed * first, (k * suffix).T, eye * (keep_row * any_first)))
    inverses = block_inverses(mats)
    for i in range(STEP_HEADS):
        cols = slice(i * width, (i + 1) * width)
        coupling_cross, reading0, reading1, reading_cross, right, query, key_end, diag = kept[i]
        u0 = mm3(inverses[2 * i], right[:half])
        u1 = mm3(inverses[2 * i + 1], right[half:] - mm3(coupling_cross, u0))
        u = jnp.concatenate([u0, u1], axis=0)
        r0 = mm3(reading0, u0)
        r1 = mm3(jnp.concatenate([reading_cross, reading1], axis=1), u)
        read = jnp.concatenate([r0, r1], axis=0)
        out_ref[:, cols] = read[:, :width]
        corr_ref[i] = (query - read[:, width:]).astype(corr_ref.dtype)
        lhs = jnp.concatenate([key_end * m for m in select], axis=0)
        states = mm1(lhs, u[:, :width])
        map_ref[i] = diag - mm1(key_end * first_row, u[:, width:])
        tail_ref[i] = states[ENDS_MAX * width:]
        end0_ref[i] = states[:width]
        for e in range(1, ENDS_MAX):
            ends_ref[e - 1, i] = states[e * width:(e + 1) * width].astype(BF16)


def local_math(q, k, v, f, rate, beta, seg, before, base, ends):
    length, total = q.shape
    heads = beta.shape[1]
    width = total // heads
    steps = heads // STEP_HEADS
    wide = pl.BlockSpec((length, STEP_HEADS * width), lambda n, s: (0, n))
    whole = lambda shape: pl.BlockSpec(shape, lambda n, s: (0, 0))
    cube = pl.BlockSpec((STEP_HEADS, width, width), lambda n, s: (n, 0, 0))
    info = jnp.stack([before, base, ends]).astype(jnp.int32)
    return pl.pallas_call(
        local_kernel,
        out_shape=(
            jax.ShapeDtypeStruct((length, total), F32),
            jax.ShapeDtypeStruct((heads, length, width), BF16),
            jax.ShapeDtypeStruct((heads, width, width), F32),
            jax.ShapeDtypeStruct((heads, width, width), F32),
            jax.ShapeDtypeStruct((heads, width, width), F32),
            jax.ShapeDtypeStruct((ENDS_MAX - 1, heads, width, width), BF16),
        ),
        grid_spec=pltpu.PrefetchScalarGridSpec(
            num_scalar_prefetch=1,
            grid=(steps,),
            in_specs=[wide, wide, wide, wide, pl.BlockSpec((1, STEP_HEADS * width), lambda n, s: (0, n)),
                      whole((length, heads)), whole((length, 1)), whole((1, length))],
            out_specs=(
                wide,
                pl.BlockSpec((STEP_HEADS, length, width), lambda n, s: (n, 0, 0)),
                cube, cube, cube,
                pl.BlockSpec((ENDS_MAX - 1, STEP_HEADS, width, width), lambda n, s: (0, n, 0, 0)),
            ),
        ),
        compiler_params=pltpu.CompilerParams(vmem_limit_bytes=48 << 20),
        name="local_math",
    )(info, q, k, v, f, rate.reshape(1, -1), beta, seg.reshape(-1, 1), seg.reshape(1, -1))


def from_behind(block, axis, distance):
    devices = range(lax.axis_size(axis))
    route = [(i - distance, i) for i in devices if i - distance in devices]
    return lax.ppermute(block, axis, route)


def per_device(query_proj, key_proj, value_proj, forget_logits, decay_rate, beta_logits,
               gate_logits, norm_gain, out_weight, stream_starts, stream_slots):
    length = query_proj.shape[0]
    heads = beta_logits.shape[1]
    width = decay_rate.shape[0] // heads
    devices = lax.axis_size("seq")
    place = lax.axis_index("seq")
    anchor = place * length
    positions = anchor + jnp.arange(length, dtype=jnp.int32)
    count = lambda mask: jnp.sum(mask.astype(jnp.int32))
    segments = jnp.sum((stream_starts[None, :] <= positions[:, None]).astype(jnp.int32), axis=1)
    before = count(stream_starts <= anchor - 1)
    before = jnp.where(place == 0, -1, before)
    later = stream_starts[1:]
    earlier = count(later <= anchor)
    ends = count((later > anchor) & (later <= anchor + length)) + (place == devices - 1).astype(jnp.int32)
    local, corr, maps, tail, end0, ends_rest = local_math(
        query_proj, key_proj, value_proj, forget_logits, decay_rate, beta_logits,
        segments, before, earlier + 1, ends)
    open_flag = (ends == 0).astype(F32)
    arriving = jnp.zeros((heads, width, width), BF16)
    maps16 = maps.astype(BF16)
    for _ in range(devices - 1):
        moved = jnp.matmul(maps16, arriving, preferred_element_type=F32)
        arriving = from_behind((tail + open_flag * moved).astype(BF16), "seq", 1)
    moved = jnp.matmul(maps16, arriving, preferred_element_type=F32)
    end0 = end0 + (1.0 - open_flag) * moved
    outputs = jnp.matmul(corr, arriving, preferred_element_type=F32).transpose(1, 0, 2) + local.reshape(length, heads, width)
    inverse_rms = lax.rsqrt(jnp.mean(outputs * outputs, axis=-1, keepdims=True) + 1e-05)
    gates = jax.nn.sigmoid(gate_logits.astype(F32).reshape(length, heads, width))
    hidden = (outputs * inverse_rms * norm_gain * gates).reshape(length, heads * width).astype(BF16)
    partial_value = jnp.dot(hidden, out_weight, preferred_element_type=F32)
    layer_out = lax.psum_scatter(partial_value.astype(BF16), ("head", "rep"), scatter_dimension=1, tiled=True)
    packed = jnp.concatenate([end0.astype(BF16)[None], ends_rest], axis=0)
    owned = stream_slots.shape[0] // devices
    ranks = jnp.arange(stream_slots.shape[0], dtype=jnp.int32) - earlier
    picks = jnp.arange(ENDS_MAX, dtype=jnp.int32)
    hit = (ranks[None, :] == picks[:, None]) & (picks < ends)[:, None]
    end_slots = jnp.sum(jnp.where(hit, stream_slots[None, :] + 1, 0), axis=1) - 1
    states = lax.all_gather(packed, "seq", axis=0, tiled=True)
    slots = lax.all_gather(end_slots, "seq", axis=0, tiled=True)
    chosen = (slots[None, :] == place * owned + jnp.arange(owned, dtype=jnp.int32)[:, None]).astype(BF16)
    slot_states = jnp.dot(chosen, states.reshape(states.shape[0], -1), preferred_element_type=F32)
    return (layer_out, slot_states.reshape(owned, heads, width, width).astype(BF16))


def solution(mesh):
    rows = P(("groups", "seq"), ("head", "rep"))
    in_specs = (rows, rows, rows, rows, P(("head", "rep")), rows, rows, P(),
                P(("head", "rep"), None), P("groups"), P("groups"))
    out_specs = (rows, P(("groups", "seq"), ("head", "rep"), None, None))
    return jax.shard_map(per_device, mesh=mesh, in_specs=in_specs, out_specs=out_specs, check_vma=False)
```

time: 426 us -> 172 us (0.40); the launches traced: 429 us -> 171 us
  other arithmetic: 178 us -> 6.14 us
  matrix products: 78.9 us -> 9.8 us
  local copies, waits for them, and re-layouts: 39 us -> 14.9 us
  Pallas kernels: 0 us -> 21 us
  loops' own time: 16.8 us -> 0 us
    another operation x10 -> x1, other arithmetic: 159 us -> 0.08 us  [local_math(): info = jnp.stack([before, base, ends]).astype(jnp.int32)]
    dot_general x41 -> x7, matrix products: 76.7 us -> 9.8 us  [the longest x1 5.31 us: per_device(): partial_value = jnp.dot(hidden, out_weight, preferred_element_type=F32)]
    pallas_call x0 -> x1, Pallas kernels: none -> 21 us  [local_math(): pl.pallas_call(local_kernel, out_shape=(jax.ShapeDtypeStruct((length, tot...]
    another operation x2 -> x0, loops' own time: 16.8 us -> none  [the longest x1 16.7 us: run_blocks(): return lax.scan(advance, starting, inputs)]
    dynamic_update_slice x4 -> x0, local copies, waits for them, and re-layouts: 8.42 us -> none  [run_blocks(): return lax.scan(advance, starting, inputs)]
    all_gather x1 -> x0, local copies, waits for them, and re-layouts: 6.62 us -> none  [per_device(): states_piece = lax.all_gather(packed, 'seq', axis=0, tiled=True)]
    while x86 -> x0, local copies, waits for them, and re-layouts: 6.02 us -> none
    mul x9 -> x0, other arithmetic: 5.8 us -> none  [the longest x2 3.06 us: advance(): value_blk * beta_blk[:, :, None]]
  transfers between devices with their start and end apart: 5 -> 5, of which waited for: 4 -> 4; matrix products, arithmetic and copies ran while one was open for 6% -> 11% of each run, Pallas kernels for 0% -> 0%
where the time goes in v1:
time: 172 us; the launch traced here: 171 us
  waiting for transfers between devices  77.4 us (45%)
  Pallas kernels  21 us (12%)
  between operations  18.3 us (11%)
  local copies, waits for them, and re-layouts  14.9 us (9%)
  starting transfers between devices  13.8 us (8%)
  matrix products  9.8 us (6%)
  blocking collectives  9.67 us (6%)
  other arithmetic  6.14 us (4%)
    all_gather x1, waiting for transfers between devices, per_device(): states = lax.all_gather(packed, 'seq', axis=0, tiled=True)  63 us
    pallas_call x1, Pallas kernels, local_math(): pl.pallas_call(local_kernel, out_shape=(jax.ShapeDtypeStruct((length, tot...  21 us
    ppermute x3, waiting for transfers between devices, from_behind(): return lax.ppermute(block, axis, route)  14.4 us
    ppermute x3, starting transfers between devices, from_behind(): return lax.ppermute(block, axis, route)  13.8 us
    unnamed x24, local copies, waits for them, and re-layouts  12.8 us
    unnamed x1, blocking collectives  9.67 us
    dot_general x1, matrix products, per_device(): partial_value = jnp.dot(hidden, out_weight, preferred_element_type=F32)  5.31 us
  transfers between devices with their start and end apart: 5, of which 4 were waited for; matrix products, arithmetic and copies ran while one was open for 11% of the time, Pallas kernels for 0%

profile of v1, /device:TPU:0, one launch (start us, length us, event | category | flops | bytes accessed | tf_op | source)
XLA Modules:
  0.0 171.0 jit_solution(15584673611073055617)
XLA Ops:
  8.0 0.0 all-gather.2.cloned.1.call-start
  8.1 1.4 fusion.20
  9.4 1.4 fusion.19
  10.8 0.8 copy.32.beta_ref
  11.6 0.7 convert_reduce_fusion
  12.4 0.1 copy.33.seg_col_ref
  14.5 0.1 pad_add_fusion.info_ref
  14.6 0.0 copy-start
  14.6 1.0 copy-done
  15.6 0.0 copy-start.1
  15.6 1.0 copy-done.1
  16.7 0.0 copy-start.2
  16.7 1.0 copy-done.2
  17.7 0.0 copy-start.3
  17.7 1.0 copy-done.3
  18.7 0.0 copy-start.4
  18.7 0.7 copy-done.4
  19.4 21.0 %local_math.1 = (f32[256,1024]{1,0:T(8,128)}, bf16[8,256,128]{2,1,0:T(8,128)(2,1)S(1)}, f32[8,128,128]{2,1,0:T(8,128)S(1)}, f32[8,128,128]{2,1,0:T(8,128)S(1)}, ...) custom-call(s32[3]{0:T(128)S(1)} %pad_add_fusion.info_ref, bf16[256,1024]{1,0:T(8,128)(2,1)S(1)} %copy-done, ...), custom_call_target="tpu_custom_call" | custom-call | tf_op jit(solution)/shard_map/local_math/pallas_call | solution.py:163
  40.5 0.0 copy-start.5
  40.5 0.2 fusion.10
  40.7 5.0 %collective-permute-start = (bf16[8,128,128]{2,1,0:T(8,128)(2,1)S(1)}, bf16[8,128,128]{2,1,0:T(8,128)(2,1)S(1)}, u32[]{:S(2)}, u32[]{:S(2)}) collective-permute-start(bf16[8,128,128]{2,1,0:T(8,128)(2,1)S(1)} %fusion.10), channel_id=1, source_target_pairs={{0,4},{4,8},{8,12},{1,5},{5,9},{9,13},{2,6},{6,10},{10,14},{3,7},{... | collective-permute-start | bytes 786440 | tf_op jit(solution)/shard_map/ppermute | solution.py:193
  45.6 5.5 %collective-permute-done = bf16[8,128,128]{2,1,0:T(8,128)(2,1)S(1)} collective-permute-done((bf16[8,128,128]{2,1,0:T(8,128)(2,1)S(1)}, bf16[8,128,128]{2,1,0:T(8,128)(2,1)S(1)}, u32[]{:S(2)}, u32[]{:S(2)}) %collective-permute-start) | collective-permute-done | bytes 262176 | tf_op jit(solution)/shard_map/ppermute | solution.py:193
  51.2 0.2 fusion.11
  51.4 4.4 %collective-permute-start.1 = (bf16[8,128,128]{2,1,0:T(8,128)(2,1)S(1)}, bf16[8,128,128]{2,1,0:T(8,128)(2,1)S(1)}, u32[]{:S(2)}, u32[]{:S(2)}) collective-permute-start(bf16[8,128,128]{2,1,0:T(8,128)(2,1)S(1)} %fusion.11), channel_id=1, source_target_pairs={{0,4},{4,8},{8,12},{1,5},{5,9},{9,13},{2,6},{6,10},{10,14},{3,7},{... | collective-permute-start | bytes 786440 | tf_op jit(solution)/shard_map/ppermute | solution.py:193
  55.8 4.7 %collective-permute-done.1 = bf16[8,128,128]{2,1,0:T(8,128)(2,1)S(1)} collective-permute-done((bf16[8,128,128]{2,1,0:T(8,128)(2,1)S(1)}, bf16[8,128,128]{2,1,0:T(8,128)(2,1)S(1)}, u32[]{:S(2)}, u32[]{:S(2)}) %collective-permute-start.1) | collective-permute-done | bytes 262176 | tf_op jit(solution)/shard_map/ppermute | solution.py:193
  60.5 0.9 fusion.12
  61.4 4.4 %collective-permute-start.2 = (bf16[8,128,128]{2,1,0:T(8,128)(2,1)}, bf16[8,128,128]{2,1,0:T(8,128)(2,1)S(1)}, u32[]{:S(2)}, u32[]{:S(2)}) collective-permute-start(bf16[8,128,128]{2,1,0:T(8,128)(2,1)} %fusion.12), channel_id=1, source_target_pairs={{0,4},{4,8},{8,12},{1,5},{5,9},{9,13},{2,6},{6,10},{10,14},{3,7},{... | collective-permute-start | bytes 786440 | tf_op jit(solution)/shard_map/ppermute | solution.py:193
  65.8 4.2 %collective-permute-done.2 = bf16[8,128,128]{2,1,0:T(8,128)(2,1)S(1)} collective-permute-done((bf16[8,128,128]{2,1,0:T(8,128)(2,1)}, bf16[8,128,128]{2,1,0:T(8,128)(2,1)S(1)}, u32[]{:S(2)}, u32[]{:S(2)}) %collective-permute-start.2) | collective-permute-done | bytes 262176 | tf_op jit(solution)/shard_map/ppermute | solution.py:193
  70.0 0.2 fusion.14
  70.2 1.1 pad_maximum_fusion
  71.3 0.0 all-gather.2.cloned.1.call-update
  71.3 0.0 copy-start.7
  71.4 0.0 reduce-scatter.2.cloned.1.call-start
  71.4 0.0 copy-done.5
  71.4 0.3 add_divide_fusion
  71.7 0.3 copy.36
  72.0 1.6 copy.41
  73.6 0.4 multiply_reduce_fusion
  74.0 0.0 copy-done.7
  74.0 0.2 multiply_convert_fusion
  74.2 0.0 copy-start.8
  74.2 0.0 copy-start.6
  74.2 5.3 %convolution_convert_fusion = bf16[256,2304]{0,1:T(8,128)(2,1)} fusion(bf16[256,1024]{0,1:T(8,128)(2,1)S(1)} %bitcast.52, bf16[1024,2304]{1,0:T(8,128)(2,1)} %param.19), kind=kOutput, calls=%fused_computation.3 | convolution fusion | flops 1208549376 | bytes 6422528 | tf_op jit(solution)/shard_map/dot_general | solution.py:227
  79.5 0.0 reduce-scatter.2.cloned.1.call-update
  79.6 0.0 copy-done.8
  79.6 0.6 dynamic-slice
  80.8 0.0 copy-done.6
  80.8 0.7 iota_subtract_fusion
  81.5 0.2 select_reduce_fusion
  81.7 0.1 add_dynamic-update-slice_fusion
  81.8 9.7 %all-reduce = s32[16]{0:T(128)S(1)} all-reduce(s32[16]{0:T(128)S(1)} %add_dynamic-update-slice_fusion), channel_id=1, replica_groups=mesh['groups'=2,'seq'=4,'head'=2,'rep'=2] {'seq'}, use_global_device_ids=true, to_apply=%add | all-reduce | flops 16 | bytes 128
  91.5 63.0 %all-gather.2.cloned.1.call-done = bf16[16,8,128,128]{3,2,1,0:T(8,128)(2,1)} async-done(((bf16[4,8,128,128]{3,2,1,0:T(8,128)(2,1)}), bf16[16,8,128,128]{3,2,1,0:T(8,128)(2,1)}) %all-gather.2.cloned.1.call-update) | async-done | bytes 4194320 | tf_op jit(solution)/shard_map/all_gather | solution.py:235
  154.4 4.9 %copy.49 = bf16[2,8,1024,128]{3,1,2,0:T(8,128)(2,1)S(1)} copy(bf16[2,8,1024,128]{3,2,1,0:T(8,128)(2,1)} %bitcast.49) | data formatting | bytes 8388608
  159.3 0.8 copy.43
  160.1 2.6 %fusion.3 = bf16[2,8,128,128]{3,0,2,1:T(2,128)(2,1)S(1)} fusion(bf16[8,128,128,16]{2,1,0,3:T(8,128)(2,1)S(1)} %bitcast.48, s32[16]{0:T(128)S(1)} %all-reduce, s32[2]{0:T(128)S(1)} %iota_add_fusion.1), kind=kOutput, calls=%fused_computation.6 | convolution fusion | flops 8650784 | bytes 4718664 | tf_op jit(solution)/shard_map/dot_general | solution.py:238
  162.7 0.9 copy.38
  163.6 0.0 reduce-scatter.2.cloned.1.call-done
  (6 shorter events, 0.1 us)
Async XLA Ops:
  8.0 146.4 %all-gather.2.cloned.1.call-start = ((), (), s32[]{:S(2)}) async-start(), calls=%async_computation.2 | async-start | bytes 5242880 | tf_op jit(solution)/shard_map/all_gather | solution.py:235
  14.6 1.0 copy-start
  15.6 1.0 copy-start.1
  16.7 1.0 copy-start.2
  17.7 1.0 copy-start.3
  18.7 0.7 copy-start.4
  40.5 31.0 %copy-start.5 = (bf16[256,1024]{1,0:T(8,128)(2,1)S(1)}, bf16[256,1024]{1,0:T(8,128)(2,1)}, u32[]{:S(2)}) copy-start(bf16[256,1024]{1,0:T(8,128)(2,1)} %param.17) | copy-start | bytes 1572868
  40.7 10.5 %collective-permute-start = (bf16[8,128,128]{2,1,0:T(8,128)(2,1)S(1)}, bf16[8,128,128]{2,1,0:T(8,128)(2,1)S(1)}, u32[]{:S(2)}, u32[]{:S(2)}) collective-permute-start(bf16[8,128,128]{2,1,0:T(8,128)(2,1)S(1)} %fusion.10), channel_id=1, source_target_pairs={{0,4},{4,8},{8,12},{1,5},{5,9},{9,13},{2,6},{6,10},{10,14},{3,7},{... | collective-permute-start | bytes 786440 | tf_op jit(solution)/shard_map/ppermute | solution.py:193
  51.4 9.1 %collective-permute-start.1 = (bf16[8,128,128]{2,1,0:T(8,128)(2,1)S(1)}, bf16[8,128,128]{2,1,0:T(8,128)(2,1)S(1)}, u32[]{:S(2)}, u32[]{:S(2)}) collective-permute-start(bf16[8,128,128]{2,1,0:T(8,128)(2,1)S(1)} %fusion.11), channel_id=1, source_target_pairs={{0,4},{4,8},{8,12},{1,5},{5,9},{9,13},{2,6},{6,10},{10,14},{3,7},{... | collective-permute-start | bytes 786440 | tf_op jit(solution)/shard_map/ppermute | solution.py:193
  61.4 8.6 %collective-permute-start.2 = (bf16[8,128,128]{2,1,0:T(8,128)(2,1)}, bf16[8,128,128]{2,1,0:T(8,128)(2,1)S(1)}, u32[]{:S(2)}, u32[]{:S(2)}) collective-permute-start(bf16[8,128,128]{2,1,0:T(8,128)(2,1)} %fusion.12), channel_id=1, source_target_pairs={{0,4},{4,8},{8,12},{1,5},{5,9},{9,13},{2,6},{6,10},{10,14},{3,7},{... | collective-permute-start | bytes 786440 | tf_op jit(solution)/shard_map/ppermute | solution.py:193
  71.3 2.6 %copy-start.7 = (f32[128]{0:T(128)S(1)}, f32[128]{0:T(128)}, u32[]{:S(2)}) copy-start(f32[128]{0:T(128)} %param.18) | copy-start | bytes 1540
  71.4 92.2 %reduce-scatter.2.cloned.1.call-start = ((), (), s32[]{:S(2)}) async-start(), calls=%async_computation.1 | async-start | bytes 1474560 | tf_op jit(solution)/shard_map/reduce_scatter | solution.py:228
  74.2 5.4 %copy-start.8 = (u32[32]{0:T(128)S(1)}, u32[32]{0:T(128)}, u32[]{:S(2)}) copy-start(u32[32]{0:T(128)} %constant.35) | copy-start | bytes 388
  74.2 6.6 %copy-start.6 = (s32[8]{0:T(128)S(1)}, s32[8]{0:T(128)}, u32[]{:S(2)}) copy-start(s32[8]{0:T(128)} %param.21) | copy-start | bytes 100
Sparse Core Ops, SparseCore 0:
  71.5 82.9 all-gather.1
Sparse Core Ops, SparseCore 1:
  79.7 27.5 reduce-scatter.1

commit v2 on v1

--- a/solution.py
+++ b/solution.py
@@ -140,15 +140,15 @@
         r0 = mm3(reading0, u0)
         r1 = mm3(jnp.concatenate([reading_cross, reading1], axis=1), u)
         read = jnp.concatenate([r0, r1], axis=0)
-        out_ref[:, cols] = read[:, :width]
+        out_ref[i] = read[:, :width]
         corr_ref[i] = (query - read[:, width:]).astype(corr_ref.dtype)
         lhs = jnp.concatenate([key_end * m for m in select], axis=0)
         states = mm1(lhs, u[:, :width])
-        map_ref[i] = diag - mm1(key_end * first_row, u[:, width:])
+        map_ref[i] = (diag - mm1(key_end * first_row, u[:, width:])).astype(map_ref.dtype)
         tail_ref[i] = states[ENDS_MAX * width:]
         end0_ref[i] = states[:width]
         for e in range(1, ENDS_MAX):
-            ends_ref[e - 1, i] = states[e * width:(e + 1) * width].astype(BF16)
+            ends_ref[i, e - 1] = states[e * width:(e + 1) * width].astype(BF16)
 
 
 def local_math(q, k, v, f, rate, beta, seg, before, base, ends):
@@ -163,12 +163,12 @@
     return pl.pallas_call(
         local_kernel,
         out_shape=(
-            jax.ShapeDtypeStruct((length, total), F32),
+            jax.ShapeDtypeStruct((heads, length, width), F32),
             jax.ShapeDtypeStruct((heads, length, width), BF16),
+            jax.ShapeDtypeStruct((heads, width, width), BF16),
             jax.ShapeDtypeStruct((heads, width, width), F32),
             jax.ShapeDtypeStruct((heads, width, width), F32),
-            jax.ShapeDtypeStruct((heads, width, width), F32),
-            jax.ShapeDtypeStruct((ENDS_MAX - 1, heads, width, width), BF16),
+            jax.ShapeDtypeStruct((heads, ENDS_MAX - 1, width, width), BF16),
         ),
         grid_spec=pltpu.PrefetchScalarGridSpec(
             num_scalar_prefetch=1,
@@ -176,10 +176,10 @@
             in_specs=[wide, wide, wide, wide, pl.BlockSpec((1, STEP_HEADS * width), lambda n, s: (0, n)),
                       whole((length, heads)), whole((length, 1)), whole((1, length))],
             out_specs=(
-                wide,
+                pl.BlockSpec((STEP_HEADS, length, width), lambda n, s: (n, 0, 0)),
                 pl.BlockSpec((STEP_HEADS, length, width), lambda n, s: (n, 0, 0)),
                 cube, cube, cube,
-                pl.BlockSpec((ENDS_MAX - 1, STEP_HEADS, width, width), lambda n, s: (0, n, 0, 0)),
+                pl.BlockSpec((STEP_HEADS, ENDS_MAX - 1, width, width), lambda n, s: (n, 0, 0, 0)),
             ),
         ),
         compiler_params=pltpu.CompilerParams(vmem_limit_bytes=48 << 20),
@@ -187,56 +187,279 @@
     )(info, q, k, v, f, rate.reshape(1, -1), beta, seg.reshape(-1, 1), seg.reshape(1, -1))
 
 
-def from_behind(block, axis, distance):
-    devices = range(lax.axis_size(axis))
-    route = [(i - distance, i) for i in devices if i - distance in devices]
-    return lax.ppermute(block, axis, route)
+def finish_kernel(n, nh, scal_ref, sel_ref, local_ref, corr_ref, map_ref, tail_ref, end0_ref, rest_ref,
+                  gate_ref, gain_ref, weight_hbm, layer_ref, slot_ref,
+                  weight, hidden, parts, sums, pair_in, cross_in, state_out, state_in, own,
+                  raw_r, raw_l, buf_r, buf_l,
+                  weight_sem, st_send, st_recv, rr_send, rr_recv, rl_send, rl_recv,
+                  r_send, r_recv, l_send, l_recv, p_send, p_recv, c_send, c_recv):
+    heads, length, width = local_ref.shape
+    owned = slot_ref.shape[0]
+    me = lax.axis_index("seq")
+    head_at = lax.axis_index("head")
+    rep_at = lax.axis_index("rep")
+    piece = layer_ref.shape[1]
+    mesh_id = pl.DeviceIdType.MESH
+    up, down, partner = {"seq": me + 1}, {"seq": me - 1}, {"rep": 1 - rep_at}
+    has_up, has_down = me < n - 1, me > 0
+    load = pltpu.make_async_copy(weight_hbm, weight, weight_sem)
+    load.start()
+
+    barrier = pltpu.get_barrier_semaphore()
+
+    @pl.when(has_up)
+    def _():
+        pl.semaphore_signal(barrier, inc=1, device_id=up, device_id_type=mesh_id)
+
+    @pl.when(has_down)
+    def _():
+        pl.semaphore_signal(barrier, inc=1, device_id=down, device_id_type=mesh_id)
+
+    pl.semaphore_signal(barrier, inc=1, device_id=partner, device_id_type=mesh_id)
+    for j in range(1, nh):
+        pl.semaphore_signal(barrier, inc=1, device_id={"head": lax.rem(head_at + j, nh)}, device_id_type=mesh_id)
+
+    inner = has_up & has_down
+
+    @pl.when(inner)
+    def _():
+        pl.semaphore_wait(barrier, nh + 2)
+
+    @pl.when(jnp.logical_not(inner))
+    def _():
+        pl.semaphore_wait(barrier, nh + 1)
+
+    def remote(src, dst, send, recv, target):
+        return pltpu.make_async_remote_copy(src_ref=src, dst_ref=dst, send_sem=send, recv_sem=recv,
+                                            device_id=target, device_id_type=mesh_id)
+
+    def state_copy(h):
+        return remote(state_out.at[h], state_in.at[h], st_send.at[h], st_recv.at[h], up)
+
+    def raw_up(h):
+        return remote(own.at[h], raw_r.at[h], rr_send.at[h], rr_recv.at[h], up)
+
+    def raw_down(h):
+        return remote(own.at[h], raw_l.at[h], rl_send.at[h], rl_recv.at[h], down)
+
+    def block_up(h, j):
+        span = pl.ds(j * owned, owned)
+        return remote(buf_r.at[h, span], buf_r.at[h, span], r_send.at[h, j], r_recv.at[h, j], up)
+
+    def block_down(h, j):
+        span = pl.ds(j * owned, owned)
+        return remote(buf_l.at[h, span], buf_l.at[h, span], l_send.at[h, j], l_recv.at[h, j], down)
+
+    def pair_copy(j):
+        return remote(parts.at[2 * j + 1 - rep_at], pair_in.at[j], p_send.at[j], p_recv.at[j], partner)
+
+    def cross_copy(j):
+        return remote(sums.at[j], cross_in.at[j], c_send.at[j], c_recv.at[j],
+                      {"head": lax.rem(head_at + j, nh)})
+
+    open_flag = scal_ref[0]
+    gain = gain_ref[...]
+
+    @pl.when(me == 0)
+    def _():
+        state_in[...] = jnp.zeros_like(state_in)
+        for h in range(heads):
+            buf_r[h, :owned] = jnp.zeros((owned, width, width), BF16)
+
+    @pl.when(me == n - 1)
+    def _():
+        for h in range(heads):
+            buf_l[h, (n - 1) * owned:] = jnp.zeros((owned, width, width), BF16)
+
+    def relay(h, carry):
+        @pl.when(has_down)
+        def _():
+            state_copy(h).wait_recv()
+
+        arriving = state_in[h]
+        moved = jnp.dot(map_ref[h], arriving, preferred_element_type=F32)
+        state_out[h] = (tail_ref[h] + open_flag * moved).astype(BF16)
+
+        @pl.when(has_up)
+        def _():
+            state_copy(h).start()
+
+        own[h, 0] = (end0_ref[h] + (1.0 - open_flag) * moved).astype(BF16)
+        own[h, 1:] = rest_ref[h]
+
+        @pl.when(me == 0)
+        def _():
+            raw_up(h).start()
+
+        @pl.when(me == n - 1)
+        def _():
+            raw_down(h).start()
+
+        out = local_ref[h] + jnp.dot(corr_ref[h], arriving, preferred_element_type=F32)
+        cols = pl.ds(pl.multiple_of(h * width, width), width)
+        scale = lax.rsqrt(jnp.mean(out * out, axis=-1, keepdims=True) + 1e-05)
+        hidden[:, cols] = (out * scale * gain * jax.nn.sigmoid(gate_ref[:, cols].astype(F32))).astype(BF16)
+        return carry
+
+    lax.fori_loop(0, heads, relay, 0)
+
+    def picked(ref, which, h, s):
+        total = sel_ref[which, 0, s] * ref[h, 0].astype(F32)
+        for e in range(1, ENDS_MAX):
+            total = total + sel_ref[which, e, s] * ref[h, e].astype(F32)
+        return total
+
+    def stage(h, at_first, raw, buf, raw_copy, block_copy, which, dests, beyond, active):
+        @pl.when(active & at_first)
+        def _():
+            raw_copy(h).wait_recv()
+
+        for j in dests:
+            mine = me == j
+            further = beyond(j)
+
+            @pl.when(active & at_first & (mine | further))
+            def _():
+                for s in range(j * owned, (j + 1) * owned):
+                    buf[h, s] = picked(raw, which, h, s).astype(BF16)
+
+            @pl.when(active & jnp.logical_not(at_first) & (mine | further))
+            def _():
+                block_copy(h, j).wait_recv()
+
+            @pl.when(active & further)
+            def _():
+                for s in range(j * owned, (j + 1) * owned):
+                    buf[h, s] = (buf[h, s].astype(F32) + picked(own, 0, h, s)).astype(BF16)
+                block_copy(h, j).start()
+
+    def exchange(h, carry):
+        stage(h, me == 1, raw_r, buf_r, raw_up, block_up, 1, range(1, n), lambda j: j > me, me >= 1)
+        stage(h, me == n - 2, raw_l, buf_l, raw_down, block_down, 2, range(n - 1), lambda j: j < me, me <= n - 2)
+        for k in range(owned):
+            s = me * owned + k
+            slot_ref[k, h] = (picked(own, 0, h, s) + buf_r[h, s].astype(F32) + buf_l[h, s].astype(F32)).astype(BF16)
+        return carry
+
+    lead = heads // 4
+    load.wait()
+    full = jnp.dot(hidden[...], weight[...], preferred_element_type=F32)
+    for d in range(2 * nh):
+        parts[d] = full[:, d * piece:(d + 1) * piece].astype(BF16)
+    for j in range(nh):
+        pair_copy(j).start()
+    lax.fori_loop(0, lead, exchange, 0)
+    for j in range(nh):
+        pair_copy(j).wait_recv()
+    for j in range(1, nh):
+        at = lax.rem(head_at + j, nh)
+        sums[j] = (parts[2 * at + rep_at].astype(F32) + pair_in[at].astype(F32)).astype(BF16)
+        cross_copy(j).start()
+    lax.fori_loop(lead, heads, exchange, 0)
+    result = parts[2 * head_at + rep_at].astype(F32) + pair_in[head_at].astype(F32)
+    for j in range(1, nh):
+        cross_copy(j).wait_recv()
+        result = result + cross_in[j].astype(F32)
+    layer_ref[...] = result.astype(BF16)
+
+    for j in range(nh):
+        pair_copy(j).wait_send()
+    for j in range(1, nh):
+        cross_copy(j).wait_send()
+
+    def drain(h, carry):
+        @pl.when(has_up)
+        def _():
+            state_copy(h).wait_send()
+
+        @pl.when(me == 0)
+        def _():
+            raw_up(h).wait_send()
+
+        @pl.when(me == n - 1)
+        def _():
+            raw_down(h).wait_send()
+
+        for j in range(1, n):
+            @pl.when((me >= 1) & (j > me))
+            def _():
+                block_up(h, j).wait_send()
+
+        for j in range(n - 1):
+            @pl.when((me <= n - 2) & (j < me))
+            def _():
+                block_down(h, j).wait_send()
+
+        return carry
+
+    lax.fori_loop(0, heads, drain, 0)
+
+
+def finish(scal, sel, local, corr, maps, tail, end0, rest, gates, gain, weight, owned):
+    n = lax.axis_size("seq")
+    nh = lax.axis_size("head")
+    heads, length, width = local.shape
+    depth, model = weight.shape
+    piece = model // (2 * nh)
+    slots = n * owned
+    vmem = pl.BlockSpec(memory_space=pltpu.VMEM)
+    smem = pl.BlockSpec(memory_space=pltpu.SMEM)
+    dma = pltpu.SemaphoreType.DMA
+    cube = pltpu.VMEM((heads, width, width), BF16)
+    quad = pltpu.VMEM((heads, ENDS_MAX, width, width), BF16)
+    flow = pltpu.VMEM((heads, slots, width, width), BF16)
+    return pl.pallas_call(
+        functools.partial(finish_kernel, n, nh),
+        out_shape=(jax.ShapeDtypeStruct((length, piece), BF16),
+                   jax.ShapeDtypeStruct((owned, heads, width, width), BF16)),
+        in_specs=[smem, smem] + [vmem] * 8 + [pl.BlockSpec(memory_space=pl.ANY)],
+        out_specs=(vmem, vmem),
+        scratch_shapes=[
+            pltpu.VMEM((depth, model), BF16),
+            pltpu.VMEM((length, depth), BF16),
+            pltpu.VMEM((2 * nh, length, piece), BF16),
+            pltpu.VMEM((nh, length, piece), BF16),
+            pltpu.VMEM((nh, length, piece), BF16),
+            pltpu.VMEM((nh, length, piece), BF16),
+            cube, cube, quad, quad, quad, flow, flow,
+            dma(()),
+            dma((heads,)), dma((heads,)), dma((heads,)), dma((heads,)), dma((heads,)), dma((heads,)),
+            dma((heads, n)), dma((heads, n)), dma((heads, n)), dma((heads, n)),
+            dma((nh,)), dma((nh,)), dma((nh,)), dma((nh,)),
+        ],
+        compiler_params=pltpu.CompilerParams(collective_id=0, has_side_effects=True,
+                                             vmem_limit_bytes=60 << 20),
+        name="finish",
+    )(scal, sel, local, corr, maps, tail, end0, rest, gates, gain.reshape(1, -1), weight)
 
 
 def per_device(query_proj, key_proj, value_proj, forget_logits, decay_rate, beta_logits,
                gate_logits, norm_gain, out_weight, stream_starts, stream_slots):
     length = query_proj.shape[0]
-    heads = beta_logits.shape[1]
-    width = decay_rate.shape[0] // heads
     devices = lax.axis_size("seq")
     place = lax.axis_index("seq")
     anchor = place * length
     positions = anchor + jnp.arange(length, dtype=jnp.int32)
-    count = lambda mask: jnp.sum(mask.astype(jnp.int32))
-    segments = jnp.sum((stream_starts[None, :] <= positions[:, None]).astype(jnp.int32), axis=1)
-    before = count(stream_starts <= anchor - 1)
-    before = jnp.where(place == 0, -1, before)
+    count = lambda mask: jnp.sum(mask.astype(jnp.int32), axis=-1)
+    segments = count(stream_starts[None, :] <= positions[:, None])
+    before = jnp.where(place == 0, -1, count(stream_starts <= anchor - 1))
     later = stream_starts[1:]
-    earlier = count(later <= anchor)
-    ends = count((later > anchor) & (later <= anchor + length)) + (place == devices - 1).astype(jnp.int32)
-    local, corr, maps, tail, end0, ends_rest = local_math(
+    spots = place + jnp.array([0, -1, 1], jnp.int32)
+    begins = spots[:, None] * length
+    earlier = count(later[None] <= begins)
+    ends = count((later[None] > begins) & (later[None] <= begins + length)) + (spots == devices - 1).astype(jnp.int32)
+    total = stream_slots.shape[0]
+    picks = jnp.arange(ENDS_MAX, dtype=jnp.int32)
+    hit = ((jnp.arange(total, dtype=jnp.int32)[None, None, :] == (earlier[:, None] + picks[None, :])[:, :, None])
+           & (picks[None, :] < ends[:, None])[:, :, None])
+    places = jnp.sum(jnp.where(hit, stream_slots[None, None, :] + 1, 0), axis=-1) - 1
+    sel = (places[:, :, None] == jnp.arange(total, dtype=jnp.int32)).astype(F32)
+    scal = (ends[:1] == 0).astype(F32)
+    local, corr, maps, tail, end0, rest = local_math(
         query_proj, key_proj, value_proj, forget_logits, decay_rate, beta_logits,
-        segments, before, earlier + 1, ends)
-    open_flag = (ends == 0).astype(F32)
-    arriving = jnp.zeros((heads, width, width), BF16)
-    maps16 = maps.astype(BF16)
-    for _ in range(devices - 1):
-        moved = jnp.matmul(maps16, arriving, preferred_element_type=F32)
-        arriving = from_behind((tail + open_flag * moved).astype(BF16), "seq", 1)
-    moved = jnp.matmul(maps16, arriving, preferred_element_type=F32)
-    end0 = end0 + (1.0 - open_flag) * moved
-    outputs = jnp.matmul(corr, arriving, preferred_element_type=F32).transpose(1, 0, 2) + local.reshape(length, heads, width)
-    inverse_rms = lax.rsqrt(jnp.mean(outputs * outputs, axis=-1, keepdims=True) + 1e-05)
-    gates = jax.nn.sigmoid(gate_logits.astype(F32).reshape(length, heads, width))
-    hidden = (outputs * inverse_rms * norm_gain * gates).reshape(length, heads * width).astype(BF16)
-    partial_value = jnp.dot(hidden, out_weight, preferred_element_type=F32)
-    layer_out = lax.psum_scatter(partial_value.astype(BF16), ("head", "rep"), scatter_dimension=1, tiled=True)
-    packed = jnp.concatenate([end0.astype(BF16)[None], ends_rest], axis=0)
-    owned = stream_slots.shape[0] // devices
-    ranks = jnp.arange(stream_slots.shape[0], dtype=jnp.int32) - earlier
-    picks = jnp.arange(ENDS_MAX, dtype=jnp.int32)
-    hit = (ranks[None, :] == picks[:, None]) & (picks < ends)[:, None]
-    end_slots = jnp.sum(jnp.where(hit, stream_slots[None, :] + 1, 0), axis=1) - 1
-    states = lax.all_gather(packed, "seq", axis=0, tiled=True)
-    slots = lax.all_gather(end_slots, "seq", axis=0, tiled=True)
-    chosen = (slots[None, :] == place * owned + jnp.arange(owned, dtype=jnp.int32)[:, None]).astype(BF16)
-    slot_states = jnp.dot(chosen, states.reshape(states.shape[0], -1), preferred_element_type=F32)
-    return (layer_out, slot_states.reshape(owned, heads, width, width).astype(BF16))
+        segments, before, earlier[0] + 1, ends[0])
+    return finish(scal, sel, local, corr, maps, tail, end0, rest, gate_logits, norm_gain, out_weight,
+                  total // devices)
 
 
 def solution(mesh):

time: 172 us -> 153 us (0.89)
  Pallas kernels: 21 us -> 130 us
  waiting for transfers between devices: 77.4 us -> 0 us
  between operations: 18.3 us -> 1.45 us
  starting transfers between devices: 13.8 us -> 0 us
  matrix products: 9.8 us -> 0 us
  blocking collectives: 9.67 us -> 0 us
    pallas_call x1 -> x2, Pallas kernels: 21 us -> 130 us  [the longest x1 110 us: finish(): pl.pallas_call(functools.partial(finish_kernel, n, nh), out_shape=(jax.Sh...]
    all_gather x1 -> x0, waiting for transfers between devices: 63 us -> none  [per_device(): states = lax.all_gather(packed, 'seq', axis=0, tiled=True)]
    ppermute x3 -> x0, waiting for transfers between devices: 14.4 us -> none  [from_behind(): return lax.ppermute(block, axis, route)]
    ppermute x3 -> x0, starting transfers between devices: 13.8 us -> none  [from_behind(): return lax.ppermute(block, axis, route)]
    dot_general x7 -> x0, matrix products: 9.8 us -> none  [the longest x1 5.31 us: per_device(): partial_value = jnp.dot(hidden, out_weight, preferred_element_type=F32)]
    unnamed x1 -> x0, blocking collectives: 9.67 us -> none
    add x1 -> x4, other arithmetic: 0.01 us -> 2.05 us  [the longest x1 0.66 us: per_device(): count((later[None] > begins) & (later[None] <= begins + length))]
    pallas_call x0 -> x1, local copies, waits for them, and re-layouts: none -> 1.84 us  [finish(): pl.pallas_call(functools.partial(finish_kernel, n, nh), out_shape=(jax.Sh...]
  transfers between devices with their start and end apart: 5 -> 0, of which waited for: 4 -> 0; matrix products, arithmetic and copies ran while one was open for 11% -> 0% of each run, Pallas kernels for 0% -> 0%
where the time goes in v2:
time: 153 us; the launch traced here: 152 us
  Pallas kernels  130 us (85%)
  local copies, waits for them, and re-layouts  15.3 us (10%)
  other arithmetic  5.38 us (4%)
    pallas_call x1, Pallas kernels, finish(): pl.pallas_call(functools.partial(finish_kernel, n, nh), out_shape=(jax.Sh...  110 us
    pallas_call x1, Pallas kernels, local_math(): pl.pallas_call(local_kernel, out_shape=(jax.ShapeDtypeStruct((heads, leng...  20.2 us
    unnamed x24, local copies, waits for them, and re-layouts  12.6 us

profile of v2, /device:TPU:0, one launch (start us, length us, event | category | flops | bytes accessed | tf_op | source)
XLA Modules:
  0.0 152.1 jit_solution(15303907173652237246)
XLA Ops:
  0.6 1.3 fusion.3
  2.6 0.7 broadcast_add_fusion.1
  3.2 0.7 slice.10
  4.0 0.7 convert_reduce_fusion
  4.7 0.7 broadcast_add_fusion.2
  5.4 0.2 convert_reduce_fusion.1
  5.6 0.7 fusion.2
  6.4 0.1 pad_add_fusion.info_ref
  6.5 0.1 iota_compare_fusion.2
  6.5 0.1 iota_add_fusion
  6.6 0.2 select_reduce_fusion
  6.8 0.7 fusion.1.sel_ref
  7.5 0.8 copy.19.beta_ref
  8.3 0.1 copy.20.seg_col_ref
  8.4 0.0 copy-start.5
  8.5 1.0 copy-done.5
  9.5 0.0 copy-start.6
  9.5 1.0 copy-done.6
  10.5 0.0 copy-start.7
  10.5 1.0 copy-done.7
  11.6 0.0 copy-start.8
  11.6 1.0 copy-done.8
  12.6 0.0 copy-start.10
  12.6 0.7 copy-done.10
  13.3 20.2 %local_math.1 = (f32[8,256,128]{2,1,0:T(8,128)S(1)}, bf16[8,256,128]{2,1,0:T(8,128)(2,1)S(1)}, bf16[8,128,128]{2,1,0:T(8,128)(2,1)S(1)}, f32[8,128,128]{2,1,0:T(...) custom-call(s32[3]{0:T(128)S(1)} %pad_add_fusion.info_ref, bf16[256,1024]{1,0:T(8,128)(2,1)S(1)} %copy-done.5, ...), custom_call_target="tpu_custom_call" | custom-call | tf_op jit(solution)/shard_map/local_math/pallas_call | solution.py:163
  33.6 0.0 copy-start
  33.6 1.0 copy-done
  34.5 0.0 copy-start.1
  34.5 0.9 copy-done.1
  35.5 0.0 copy-start.2
  35.5 0.8 copy-done.2
  36.3 0.0 copy-start.3
  36.3 0.8 copy-done.3
  37.1 0.0 copy-start.4
  37.1 0.8 copy-done.4
  37.9 0.0 copy-start.9
  37.9 0.7 copy-done.9
  38.6 109.7 %finish.1 = (bf16[256,576]{1,0:T(8,128)(2,1)}, bf16[2,8,128,128]{3,2,1,0:T(8,128)(2,1)}) custom-call(f32[1]{0:T(128)S(6)} %convert_element_type.23.scal_ref, f32[3,4,8]{2,1,0:T(4,128)} %fusion.1.sel_ref, f32[8,256,128]{2,1,0:T(8,128)} %copy-done, bf16[8,256,128]{2,1,0:T(8,128)(2,1)} %copy-done.2, bf16[8,128,128]{2,1,0:T(8,128)(2,1)} %copy-done.9, ...), custom_call_target="tpu_custom_call" | custom-call | tf_op jit(solution)/shard_map/finish/pallas_call | solution.py:411
  148.3 1.8 %copy.21 = bf16[256,576]{0,1:T(8,128)(2,1)} copy(bf16[256,576]{1,0:T(8,128)(2,1)} %get-tuple-element.18) | data formatting | bytes 589824 | tf_op jit(solution)/shard_map/finish/pallas_call | solution.py:411
  150.2 1.9 %copy.23 = bf16[2,8,128,128]{3,2,1,0:T(8,128)(2,1)} copy(bf16[2,8,128,128]{3,2,1,0:T(8,128)(2,1)} %get-tuple-element.27) | data formatting | bytes 1048576
  (2 shorter events, 0.0 us)
Async XLA Ops:
  8.4 1.0 copy-start.5
  9.5 1.0 copy-start.6
  10.5 1.0 copy-start.7
  11.6 1.0 copy-start.8
  12.6 0.7 copy-start.10
  33.6 1.0 copy-start
  34.5 0.9 copy-start.1
  35.5 0.8 copy-start.2
  36.3 0.8 copy-start.3
  37.1 0.8 copy-start.4
  37.9 0.7 copy-start.9

commit v3 on v2

--- a/solution.py
+++ b/solution.py
@@ -187,11 +187,15 @@
     )(info, q, k, v, f, rate.reshape(1, -1), beta, seg.reshape(-1, 1), seg.reshape(1, -1))
 
 
-def finish_kernel(n, nh, scal_ref, sel_ref, local_ref, corr_ref, map_ref, tail_ref, end0_ref, rest_ref,
-                  gate_ref, gain_ref, weight_hbm, layer_ref, slot_ref,
-                  weight, hidden, parts, sums, pair_in, cross_in, state_out, state_in, own,
+LAG = 2
+
+
+def finish_kernel(n, nh, scal_ref, sel_ref, gain_ref, local_hbm, corr_hbm, map_hbm, tail_hbm, end0_hbm, rest_hbm,
+                  gate_hbm, weight_hbm, layer_ref, slot_ref,
+                  local_ref, corr_ref, map_ref, tail_ref, end0_ref, gate_ref, weight, hidden, parts, sums, pair_in, cross_in, state_out, state_in, own,
                   raw_r, raw_l, buf_r, buf_l,
-                  weight_sem, st_send, st_recv, rr_send, rr_recv, rl_send, rl_recv,
+                  load_sem, st_send, st_recv, rr_send, rr_recv, rl_send, rl_recv,
+                  qr_send, qr_recv, ql_send, ql_recv,
                   r_send, r_recv, l_send, l_recv, p_send, p_recv, c_send, c_recv):
     heads, length, width = local_ref.shape
     owned = slot_ref.shape[0]
@@ -202,8 +206,12 @@
     mesh_id = pl.DeviceIdType.MESH
     up, down, partner = {"seq": me + 1}, {"seq": me - 1}, {"rep": 1 - rep_at}
     has_up, has_down = me < n - 1, me > 0
-    load = pltpu.make_async_copy(weight_hbm, weight, weight_sem)
-    load.start()
+    pairs = ((rest_hbm, own.at[:, pl.ds(1, ENDS_MAX - 1)]), (map_hbm, map_ref), (tail_hbm, tail_ref),
+             (end0_hbm, end0_ref), (local_hbm, local_ref), (corr_hbm, corr_ref), (gate_hbm, gate_ref),
+             (weight_hbm, weight))
+    loads = [pltpu.make_async_copy(src, dst, load_sem.at[i]) for i, (src, dst) in enumerate(pairs)]
+    for load in loads:
+        load.start()
 
     barrier = pltpu.get_barrier_semaphore()
 
@@ -237,10 +245,18 @@
         return remote(state_out.at[h], state_in.at[h], st_send.at[h], st_recv.at[h], up)
 
     def raw_up(h):
-        return remote(own.at[h], raw_r.at[h], rr_send.at[h], rr_recv.at[h], up)
+        return remote(own.at[h, pl.ds(0, 1)], raw_r.at[h, pl.ds(0, 1)], rr_send.at[h], rr_recv.at[h], up)
 
     def raw_down(h):
-        return remote(own.at[h], raw_l.at[h], rl_send.at[h], rl_recv.at[h], down)
+        return remote(own.at[h, pl.ds(0, 1)], raw_l.at[h, pl.ds(0, 1)], rl_send.at[h], rl_recv.at[h], down)
+
+    others = pl.ds(1, ENDS_MAX - 1)
+
+    def others_up(h):
+        return remote(own.at[h, others], raw_r.at[h, others], qr_send.at[h], qr_recv.at[h], up)
+
+    def others_down(h):
+        return remote(own.at[h, others], raw_l.at[h, others], ql_send.at[h], ql_recv.at[h], down)
 
     def block_up(h, j):
         span = pl.ds(j * owned, owned)
@@ -271,6 +287,23 @@
         for h in range(heads):
             buf_l[h, (n - 1) * owned:] = jnp.zeros((owned, width, width), BF16)
 
+    loads[0].wait()
+
+    def early(h, carry):
+        @pl.when(me == 0)
+        def _():
+            others_up(h).start()
+
+        @pl.when(me == n - 1)
+        def _():
+            others_down(h).start()
+
+        return carry
+
+    lax.fori_loop(0, heads, early, 0)
+    for load in loads[1:-1]:
+        load.wait()
+
     def relay(h, carry):
         @pl.when(has_down)
         def _():
@@ -285,7 +318,6 @@
             state_copy(h).start()
 
         own[h, 0] = (end0_ref[h] + (1.0 - open_flag) * moved).astype(BF16)
-        own[h, 1:] = rest_ref[h]
 
         @pl.when(me == 0)
         def _():
@@ -309,9 +341,10 @@
             total = total + sel_ref[which, e, s] * ref[h, e].astype(F32)
         return total
 
-    def stage(h, at_first, raw, buf, raw_copy, block_copy, which, dests, beyond, active):
+    def stage(h, at_first, raw, buf, raw_copy, others_copy, block_copy, which, dests, beyond, active):
         @pl.when(active & at_first)
         def _():
+            others_copy(h).wait_recv()
             raw_copy(h).wait_recv()
 
         for j in dests:
@@ -333,16 +366,31 @@
                     buf[h, s] = (buf[h, s].astype(F32) + picked(own, 0, h, s)).astype(BF16)
                 block_copy(h, j).start()
 
-    def exchange(h, carry):
-        stage(h, me == 1, raw_r, buf_r, raw_up, block_up, 1, range(1, n), lambda j: j > me, me >= 1)
-        stage(h, me == n - 2, raw_l, buf_l, raw_down, block_down, 2, range(n - 1), lambda j: j < me, me <= n - 2)
-        for k in range(owned):
-            s = me * owned + k
-            slot_ref[k, h] = (picked(own, 0, h, s) + buf_r[h, s].astype(F32) + buf_l[h, s].astype(F32)).astype(BF16)
+    def exchange(t, carry):
+        hr = t - LAG * (me - 1)
+        hl = t - LAG * (n - 2 - me)
+        hf = t - LAG * (n - 2)
+
+        @pl.when((me >= 1) & (hr >= 0) & (hr < heads))
+        def _():
+            stage(hr, me == 1, raw_r, buf_r, raw_up, others_up, block_up, 1, range(1, n), lambda j: j > me, me >= 1)
+
+        @pl.when((me <= n - 2) & (hl >= 0) & (hl < heads))
+        def _():
+            stage(hl, me == n - 2, raw_l, buf_l, raw_down, others_down, block_down, 2, range(n - 1),
+                  lambda j: j < me, me <= n - 2)
+
+        @pl.when((hf >= 0) & (hf < heads))
+        def _():
+            for k in range(owned):
+                s = me * owned + k
+                slot_ref[k, hf] = (picked(own, 0, hf, s) + buf_r[hf, s].astype(F32)
+                                   + buf_l[hf, s].astype(F32)).astype(BF16)
+
         return carry
 
-    lead = heads // 4
-    load.wait()
+    lead = max(heads // 4, 1)
+    loads[-1].wait()
     full = jnp.dot(hidden[...], weight[...], preferred_element_type=F32)
     for d in range(2 * nh):
         parts[d] = full[:, d * piece:(d + 1) * piece].astype(BF16)
@@ -355,7 +403,7 @@
         at = lax.rem(head_at + j, nh)
         sums[j] = (parts[2 * at + rep_at].astype(F32) + pair_in[at].astype(F32)).astype(BF16)
         cross_copy(j).start()
-    lax.fori_loop(lead, heads, exchange, 0)
+    lax.fori_loop(lead, heads + LAG * (n - 2), exchange, 0)
     result = parts[2 * head_at + rep_at].astype(F32) + pair_in[head_at].astype(F32)
     for j in range(1, nh):
         cross_copy(j).wait_recv()
@@ -375,10 +423,12 @@
         @pl.when(me == 0)
         def _():
             raw_up(h).wait_send()
+            others_up(h).wait_send()
 
         @pl.when(me == n - 1)
         def _():
             raw_down(h).wait_send()
+            others_down(h).wait_send()
 
         for j in range(1, n):
             @pl.when((me >= 1) & (j > me))
@@ -412,9 +462,15 @@
         functools.partial(finish_kernel, n, nh),
         out_shape=(jax.ShapeDtypeStruct((length, piece), BF16),
                    jax.ShapeDtypeStruct((owned, heads, width, width), BF16)),
-        in_specs=[smem, smem] + [vmem] * 8 + [pl.BlockSpec(memory_space=pl.ANY)],
+        in_specs=[smem, smem, vmem] + [pl.BlockSpec(memory_space=pl.ANY)] * 8,
         out_specs=(vmem, vmem),
         scratch_shapes=[
+            pltpu.VMEM(local.shape, F32),
+            pltpu.VMEM(corr.shape, BF16),
+            pltpu.VMEM(maps.shape, BF16),
+            pltpu.VMEM(tail.shape, F32),
+            pltpu.VMEM(end0.shape, F32),
+            pltpu.VMEM(gates.shape, BF16),
             pltpu.VMEM((depth, model), BF16),
             pltpu.VMEM((length, depth), BF16),
             pltpu.VMEM((2 * nh, length, piece), BF16),
@@ -422,7 +478,8 @@
             pltpu.VMEM((nh, length, piece), BF16),
             pltpu.VMEM((nh, length, piece), BF16),
             cube, cube, quad, quad, quad, flow, flow,
-            dma(()),
+            dma((8,)),
+            dma((heads,)), dma((heads,)), dma((heads,)), dma((heads,)),
             dma((heads,)), dma((heads,)), dma((heads,)), dma((heads,)), dma((heads,)), dma((heads,)),
             dma((heads, n)), dma((heads, n)), dma((heads, n)), dma((heads, n)),
             dma((nh,)), dma((nh,)), dma((nh,)), dma((nh,)),
@@ -430,7 +487,7 @@
         compiler_params=pltpu.CompilerParams(collective_id=0, has_side_effects=True,
                                              vmem_limit_bytes=60 << 20),
         name="finish",
-    )(scal, sel, local, corr, maps, tail, end0, rest, gates, gain.reshape(1, -1), weight)
+    )(scal, sel, gain.reshape(1, -1), local, corr, maps, tail, end0, rest, gates, weight)
 
 
 def per_device(query_proj, key_proj, value_proj, forget_logits, decay_rate, beta_logits,

time: 153 us -> 110 us (0.72)
  Pallas kernels: 130 us -> 87.1 us
    pallas_call x1, Pallas kernels: 110 us -> 66.8 us  [finish(): pl.pallas_call(functools.partial(finish_kernel, n, nh), out_shape=(jax.Sh...]
where the time goes in v3:
time: 110 us; the launch traced here: 109 us
  Pallas kernels  87.1 us (79%)
  local copies, waits for them, and re-layouts  15.3 us (14%)
  other arithmetic  5.38 us (5%)
  between operations  1.45 us (1%)
    pallas_call x1, Pallas kernels, finish(): pl.pallas_call(functools.partial(finish_kernel, n, nh), out_shape=(jax.Sh...  66.8 us
    pallas_call x1, Pallas kernels, local_math(): pl.pallas_call(local_kernel, out_shape=(jax.ShapeDtypeStruct((heads, leng...  20.2 us
    unnamed x24, local copies, waits for them, and re-layouts  12.6 us
    reduce_sum x3, other arithmetic, per_device(): count = lambda mask: jnp.sum(mask.astype(jnp.int32), axis=-1)  2.25 us

profile of v3, /device:TPU:0, one launch (start us, length us, event | category | flops | bytes accessed | tf_op | source)
XLA Modules:
  0.0 109.2 jit_solution(1211168999044714484)
XLA Ops:
  0.6 1.3 %fusion.3 = s32[]{:T(128)} fusion(s32[8]{0:T(128)} %param.21, s32[]{:T(128)S(6)} %sub.7), kind=kLoop, calls=%fused_computation.16 | loop fusion | flops 23 | bytes 40 | tf_op jit(solution)/shard_map/reduce_sum | solution.py:500
  2.6 0.7 broadcast_add_fusion.1
  3.2 0.7 slice.10
  4.0 0.7 convert_reduce_fusion
  4.7 0.7 broadcast_add_fusion.2
  5.4 0.2 convert_reduce_fusion.1
  5.6 0.7 fusion.2
  6.4 0.1 pad_add_fusion.info_ref
  6.5 0.1 iota_compare_fusion.2
  6.5 0.1 iota_add_fusion
  6.6 0.2 select_reduce_fusion
  6.8 0.7 fusion.1.sel_ref
  7.5 0.8 copy.19.beta_ref
  8.3 0.1 copy.20.seg_col_ref
  8.4 0.0 copy-start.5
  8.5 1.0 copy-done.5
  9.5 0.0 copy-start.6
  9.5 1.0 copy-done.6
  10.5 0.0 copy-start.7
  10.5 1.0 copy-done.7
  11.6 0.0 copy-start.8
  11.6 1.0 copy-done.8
  12.6 0.0 copy-start.10
  12.6 0.7 copy-done.10
  13.3 20.2 %local_math.1 = (f32[8,256,128]{2,1,0:T(8,128)S(1)}, bf16[8,256,128]{2,1,0:T(8,128)(2,1)S(1)}, bf16[8,128,128]{2,1,0:T(8,128)(2,1)S(1)}, f32[8,128,128]{2,1,0:T(...) custom-call(s32[3]{0:T(128)S(1)} %pad_add_fusion.info_ref, bf16[256,1024]{1,0:T(8,128)(2,1)S(1)} %copy-done.5, ...), custom_call_target="tpu_custom_call" | custom-call | tf_op jit(solution)/shard_map/local_math/pallas_call | solution.py:163
  33.6 0.0 copy-start
  33.6 1.0 copy-done
  34.5 0.0 copy-start.1
  34.5 0.9 copy-done.1
  35.5 0.0 copy-start.2
  35.5 0.8 copy-done.2
  36.3 0.0 copy-start.3
  36.3 0.8 copy-done.3
  37.1 0.0 copy-start.4
  37.1 0.8 copy-done.4
  37.9 0.0 copy-start.9
  37.9 0.7 copy-done.9
  38.6 66.8 %finish.1 = (bf16[256,576]{1,0:T(8,128)(2,1)}, bf16[2,8,128,128]{3,2,1,0:T(8,128)(2,1)}) custom-call(f32[1]{0:T(128)S(6)} %convert_element_type.23.scal_ref, f32[3,4,8]{2,1,0:T(4,128)} %fusion.1.sel_ref, f32[1,128]{1,0:T(1,128)} %bitcast.13, f32[8,256,128]{2,1,0:T(8,128)} %copy-done, bf16[8,256,128]{2,1,0:T(8,128)(2,1)} %copy-done.2, ...), custom_call_target="tpu_custom_call" | custom-call | tf_op jit(solution)/shard_map/finish/pallas_call | solution.py:461
  105.5 1.8 %copy.21 = bf16[256,576]{0,1:T(8,128)(2,1)} copy(bf16[256,576]{1,0:T(8,128)(2,1)} %get-tuple-element.18) | data formatting | bytes 589824 | tf_op jit(solution)/shard_map/finish/pallas_call | solution.py:461
  107.3 1.9 %copy.23 = bf16[2,8,128,128]{3,2,1,0:T(8,128)(2,1)} copy(bf16[2,8,128,128]{3,2,1,0:T(8,128)(2,1)} %get-tuple-element.27) | data formatting | bytes 1048576
  (2 shorter events, 0.0 us)
Async XLA Ops:
  8.4 1.0 copy-start.5
  9.5 1.0 copy-start.6
  10.5 1.0 copy-start.7
  11.6 1.0 copy-start.8
  12.6 0.7 copy-start.10
  33.6 1.0 copy-start
  34.5 0.9 copy-start.1
  35.5 0.8 copy-start.2
  36.3 0.8 copy-start.3
  37.1 0.8 copy-start.4
  37.9 0.7 copy-start.9
